TPU v7x, 512 devices: a whole 4x4x16 slice. The times are simulated.
512 devices in a mesh: blk: 32 (over y_lo, z), gy: 4 (over x), rep: 4 (over y_hi, core).
Axes of the slice: x: 4, y: 4 (y_hi: 2, y_lo: 2; y = y_hi * 2 + y_lo), z: 16, core: 2. Of those that a mesh axis runs over, the one named last changes fastest.
Arguments:
- grain_id: int32 [128, 32, 512], P('blk', 'gy', 'rep'), may hold values from 0 to 255
- init_masks: int32 [2, 128, 32, 512], P(None, 'blk', 'gy', 'rep'), may hold values from 0 to 1, as said below
- target_masks: int32 [2, 128, 32, 512], P(None, 'blk', 'gy', 'rep'), may hold values from 0 to 1, as said below
- emb_table: bfloat16 [256, 8], replicated, may hold values from -6 to 6
- w_in: float32 [64, 10], P('rep'), may hold values from -2 to 2
- b_in: float32 [64], P('rep'), may hold values from -3 to 3
- w_mid: float32 [64, 64], P('rep'), may hold values from -0.75 to 0.75
- b_mid: float32 [64], P('rep'), may hold values from -3 to 3
- w_out: float32 [6, 64], P(None, 'rep'), may hold values from -0.75 to 0.75
- b_out: float32 [6], replicated, may hold values from -4 to 4
Outputs:
- final_state: float32 [2, 128, 32, 512], P(None, 'blk', 'gy', 'rep')
- loss: float32 [], replicated
- grad_w_in: float32 [64, 10], P('rep')
- grad_b_in: float32 [64], P('rep')
- grad_w_mid: float32 [64, 64], P('rep')
- grad_b_mid: float32 [64], P('rep')
- grad_w_out: float32 [6, 64], P(None, 'rep')
- grad_b_out: float32 [6], replicated
- start_sensitivity: float32 [2, 128, 32, 512], P(None, 'blk', 'gy', 'rep')
Inputs may be any that keep to these rules, and one draw needn't show every extreme that they name: `init_masks`: 0 or 1 in every cell. `target_masks`: 0 or 1 in every cell.
All inputs are finite; a program needn't handle non-finite values.
Results may differ from a plain program's by a relative error of at most 0.0054.
The roundings to bfloat16 on the way count: a program that leaves them out, or rounds other values in their place, can miss the bound.
Values may be sent and summed in bfloat16 or wider, within the bound.
A program may use at most 64 MiB of HBM per device.

v0:
```python
import jax
import jax.numpy as jnp
from jax import lax
from jax.sharding import PartitionSpec as P

STEPS = 4
RATE_MAX = 0.15
AXES = (("rep", 3), ("gy", 2), ("blk", 1))


def ring_perms(axis):
    count = lax.axis_size(axis)
    forward = [(i, (i + 1) % count) for i in range(count)]
    backward = [((i + 1) % count, i) for i in range(count)]
    return (forward, backward)


def exchange_faces(fields):
    faces = []
    for direction, (axis, dim) in enumerate(AXES):
        block = fields[direction]
        forward, backward = ring_perms(axis)
        size = block.shape[dim]
        low = lax.ppermute(lax.slice_in_dim(block, size - 1, size, axis=dim), axis, forward)
        high = lax.ppermute(lax.slice_in_dim(block, 0, 1, axis=dim), axis, backward)
        faces.append((low, high))
    return faces


def shifted(block, low, high, dim, offset):
    size = block.shape[dim]
    if offset == 1:
        return jnp.concatenate([lax.slice_in_dim(block, 1, size, axis=dim), high], axis=dim)
    return jnp.concatenate([low, lax.slice_in_dim(block, 0, size - 1, axis=dim)], axis=dim)


def diffuse(field, field_faces, rates, rate_faces):
    summed = field
    for direction, (axis, dim) in enumerate(AXES):
        rate_here = rates[direction::3]
        for offset in (1, -1):
            low, high = field_faces[direction]
            rlow, rhigh = rate_faces[direction]
            rate_next = shifted(rate_here, rlow, rhigh, dim, offset)
            summed = summed + 0.5 * (rate_here + rate_next) * (
                shifted(field, low, high, dim, offset) - field
            )
    return summed


def rate_cotangent(state, state_faces, adjoint, adjoint_faces):
    pieces_list = []
    for direction, (axis, dim) in enumerate(AXES):
        summed = jnp.zeros_like(state)
        for offset in (1, -1):
            slow, shigh = state_faces[direction]
            alow, ahigh = adjoint_faces[direction]
            summed = summed + (shifted(state, slow, shigh, dim, offset) - state) * (
                shifted(adjoint, alow, ahigh, dim, offset) - adjoint
            )
        pieces_list.append(-0.5 * summed)
    stacked = jnp.stack(pieces_list, axis=1)
    return stacked.reshape((6,) + stacked.shape[2:])


def embed_lookup(emb_table, grain_flat):
    table_rows = emb_table.shape[0]
    one_hot = (grain_flat[None, :] == lax.broadcasted_iota(jnp.int32, (table_rows, 1), 0)).astype(
        jnp.bfloat16
    )
    looked = jnp.dot(emb_table.T, one_hot, preferred_element_type=jnp.float32)
    return looked.astype(jnp.bfloat16)


def forward_layers(params, features):
    w_in, b_in, w_mid, b_mid, w_out, b_out = params
    act_one = jnp.tanh(
        jnp.dot(w_in, features, preferred_element_type=jnp.float32)
        + b_in.astype(jnp.float32)[:, None]
    )
    hid_one = act_one.astype(jnp.bfloat16)
    act_two = jnp.tanh(
        jnp.dot(w_mid, hid_one, preferred_element_type=jnp.float32)
        + b_mid.astype(jnp.float32)[:, None]
    )
    hid_two = act_two.astype(jnp.bfloat16)
    logits = (
        jnp.dot(w_out, hid_two, preferred_element_type=jnp.float32)
        + b_out.astype(jnp.float32)[:, None]
    )
    return (RATE_MAX * jax.nn.sigmoid(logits), act_one, hid_one, act_two, hid_two)


def backward_layers(params, features, rate_grad, forward_values):
    w_in, b_in, w_mid, b_mid, w_out, b_out = params
    rate_values, act_one, hid_one, act_two, hid_two = forward_values
    out_grad = (rate_grad * rate_values * (1.0 - rate_values / RATE_MAX)).astype(jnp.bfloat16)
    two_grad = (
        jnp.dot(w_out.T, out_grad, preferred_element_type=jnp.float32) * (1.0 - act_two * act_two)
    ).astype(jnp.bfloat16)
    one_grad = (
        jnp.dot(w_mid.T, two_grad, preferred_element_type=jnp.float32) * (1.0 - act_one * act_one)
    ).astype(jnp.bfloat16)
    grad_terms = (
        jnp.dot(one_grad, features.T, preferred_element_type=jnp.float32),
        jnp.sum(one_grad, axis=1, dtype=jnp.float32),
        jnp.dot(two_grad, hid_one.T, preferred_element_type=jnp.float32),
        jnp.sum(two_grad, axis=1, dtype=jnp.float32),
        jnp.dot(out_grad, hid_two.T, preferred_element_type=jnp.float32),
        jnp.sum(out_grad, axis=1, dtype=jnp.float32),
    )
    state_grad = jnp.dot(w_in[:, -2:].T, one_grad, preferred_element_type=jnp.float32)
    return (grad_terms, state_grad)


def gather_params(w_in, b_in, w_mid, b_mid, w_out, b_out):
    n_in = w_in.shape[1]
    n_mid = w_mid.shape[1]
    packed = jnp.concatenate([w_in, b_in[:, None], w_mid, b_mid[:, None], w_out.T], axis=1).astype(
        jnp.bfloat16
    )
    full = lax.all_gather(packed, "rep", axis=0, tiled=True)
    col = 0
    w_in_b = full[:, col : col + n_in]
    col += n_in
    b_in_b = full[:, col]
    col += 1
    w_mid_b = full[:, col : col + n_mid]
    col += n_mid
    b_mid_b = full[:, col]
    col += 1
    w_out_b = full[:, col:].T
    return (w_in_b, b_in_b, w_mid_b, b_mid_b, w_out_b, b_out.astype(jnp.bfloat16))


def per_device(
    grain_id, init_masks, target_masks, emb_table, w_in, b_in, w_mid, b_mid, w_out, b_out
):
    params = gather_params(w_in, b_in, w_mid, b_mid, w_out, b_out)
    depth_cells, row_cells, col_cells = grain_id.shape
    cell_count = depth_cells * row_cells * col_cells
    block_shape = (depth_cells, row_cells, col_cells)
    embedding = embed_lookup(emb_table, grain_id.reshape(cell_count))
    state_now = init_masks.astype(jnp.float32)
    history = []
    for step_index in range(STEPS):
        features = jnp.concatenate(
            [embedding, state_now.reshape(2, cell_count).astype(jnp.bfloat16)], axis=0
        )
        rate_values = forward_layers(params, features)[0].reshape((6,) + block_shape)
        faces = exchange_faces(
            [jnp.concatenate([state_now, rate_values[d::3]], axis=0) for d in range(3)]
        )
        state_faces = [(low[:2], high[:2]) for low, high in faces]
        rate_faces = [(low[2:], high[2:]) for low, high in faces]
        history.append((state_now, state_faces, rate_values, rate_faces))
        state_now = diffuse(state_now, state_faces, rate_values, rate_faces)
    misfit = state_now - target_masks.astype(jnp.float32)
    total_cells = float(
        cell_count * lax.axis_size("blk") * lax.axis_size("gy") * lax.axis_size("rep")
    )
    loss_part = jnp.sum(misfit * misfit) / (4.0 * total_cells)
    adjoint = misfit / (2.0 * total_cells)
    grad_sums = None
    for step_index in reversed(range(STEPS)):
        state_t, state_faces, rate_values, rate_faces = history[step_index]
        adjoint_faces = exchange_faces([adjoint] * 3)
        rate_grad = rate_cotangent(state_t, state_faces, adjoint, adjoint_faces).reshape(
            6, cell_count
        )
        features = jnp.concatenate(
            [embedding, state_t.reshape(2, cell_count).astype(jnp.bfloat16)], axis=0
        )
        forward_values = forward_layers(params, features)
        step_terms, state_grad = backward_layers(params, features, rate_grad, forward_values)
        if grad_sums is None:
            grad_sums = step_terms
        else:
            grad_sums = tuple(
                (earlier + later_term for earlier, later_term in zip(grad_sums, step_terms))
            )
        adjoint = diffuse(adjoint, adjoint_faces, rate_values, rate_faces) + state_grad.reshape(
            (2,) + block_shape
        )
    start_sensitivity = adjoint * (2.0 * total_cells)
    pieces = list(grad_sums) + [loss_part[None]]
    flat = jnp.concatenate([piece.reshape(-1) for piece in pieces])
    summed_flat = lax.psum(flat, ("blk", "gy", "rep"))
    summed = []
    start = 0
    for piece in pieces:
        summed.append(summed_flat[start : start + piece.size].reshape(piece.shape))
        start += piece.size
    position = lax.axis_index("rep")
    share_width = w_in.shape[0]
    grad_w_in = lax.dynamic_slice_in_dim(summed[0], position * share_width, share_width, 0)
    grad_b_in = lax.dynamic_slice_in_dim(summed[1], position * share_width, share_width, 0)
    grad_w_mid = lax.dynamic_slice_in_dim(summed[2], position * share_width, share_width, 0)
    grad_b_mid = lax.dynamic_slice_in_dim(summed[3], position * share_width, share_width, 0)
    grad_w_out = lax.dynamic_slice_in_dim(summed[4], position * share_width, share_width, 1)
    grad_b_out = summed[5]
    loss_total = summed[6][0]
    return (
        state_now,
        loss_total,
        grad_w_in,
        grad_b_in,
        grad_w_mid,
        grad_b_mid,
        grad_w_out,
        grad_b_out,
        start_sensitivity,
    )


def solution(mesh):
    in_specs = (
        P("blk", "gy", "rep"),
        P(None, "blk", "gy", "rep"),
        P(None, "blk", "gy", "rep"),
        P(),
        P("rep", None),
        P("rep"),
        P("rep", None),
        P("rep"),
        P(None, "rep"),
        P(),
    )
    out_specs = (
        P(None, "blk", "gy", "rep"),
        P(),
        P("rep", None),
        P("rep"),
        P("rep", None),
        P("rep"),
        P(None, "rep"),
        P(),
        P(None, "blk", "gy", "rep"),
    )
    return jax.shard_map(
        per_device, mesh=mesh, in_specs=in_specs, out_specs=out_specs, check_vma=False
    )
```

profile of v0, /device:TPU:1, one launch (start us, length us, event | category | flops | bytes accessed | tf_op | source)
XLA Modules:
  0.0 383.7 jit_solution(16146299786309421557)
XLA Ops:
  5.6 13.3 %all_gather.3 = bf16[64,82]{1,0:T(8,128)(2,1)S(1)} all-gather(bf16[16,82]{1,0:T(8,128)(2,1)S(1)} %concatenate.347), channel_id=1, replica_groups=mesh['blk'=32,'gy'=4,'rep'=4] {'rep'}, dimensions={0}, use_global_device_ids=true | all-gather | bytes 13120 | tf_op jit(solution)/shard_map/all_gather | solution.py:122
  25.0 1.9 collective-permute-start.2
  26.9 3.4 collective-permute-start.3
  30.3 7.8 %collective-permute-start.4 = (f32[4,1,8,128]{3,2,1,0:T(8,128)S(1)}, f32[4,1,8,128]{3,2,1,0:T(8,128)S(1)}, u32[]{:S(2)}, u32[]{:S(2)}) collective-permute-start(f32[4,1,8,128]{3,2,1,0:T(8,128)S(1)} %get-tuple-element.85), channel_id=1, source_target_pairs={{16,0},{32,16},{48,32},{64,48},{80,64},{96,80},{112,96},{128,112},... | collective-permute-start | bytes 49160 | tf_op jit(solution)/shard_map/ppermute | solution.py:25
  38.1 1.9 collective-permute-start.5
  40.1 2.7 collective-permute-start
  43.1 4.2 %collective-permute-done = f32[4,4,8,1]{3,2,1,0:T(8,128)S(1)} collective-permute-done((f32[4,4,8,1]{3,2,1,0:T(8,128)S(1)}, f32[4,4,8,1]{3,2,1,0:T(8,128)S(1)}, u32[]{:S(2)}, u32[]{:S(2)}) %collective-permute-start) | collective-permute-done | bytes 544 | tf_op jit(solution)/shard_map/ppermute | solution.py:25
  54.9 5.5 %collective-permute-start.6 = (f32[4,4,8,1]{3,2,1,0:T(8,128)S(1)}, f32[4,4,8,1]{3,2,1,0:T(8,128)S(1)}, u32[]{:S(2)}, u32[]{:S(2)}) collective-permute-start(f32[4,4,8,1]{3,2,1,0:T(8,128)S(1)} %get-tuple-element.69), channel_id=1, source_target_pairs={{1,0},{2,1},{3,2},{0,3},{5,4},{6,5},{7,6},{4,7},{9,8},{10,9},{11,1... | collective-permute-start | bytes 1544 | tf_op jit(solution)/shard_map/ppermute | solution.py:25
  60.4 4.6 %collective-permute-start.8 = (f32[4,4,1,128]{3,2,1,0:T(1,128)S(1)}, f32[4,4,1,128]{3,2,1,0:T(1,128)S(1)}, u32[]{:S(2)}, u32[]{:S(2)}) collective-permute-start(f32[4,4,1,128]{3,2,1,0:T(1,128)S(1)} %get-tuple-element.73), channel_id=1, source_target_pairs={{4,0},{8,4},{12,8},{0,12},{5,1},{9,5},{13,9},{1,13},{6,2},{10,6},{... | collective-permute-start | bytes 24584 | tf_op jit(solution)/shard_map/ppermute | solution.py:25
  65.0 1.9 collective-permute-start.9
  66.9 4.9 %collective-permute-start.10 = (f32[4,1,8,128]{3,2,1,0:T(8,128)S(1)}, f32[4,1,8,128]{3,2,1,0:T(8,128)S(1)}, u32[]{:S(2)}, u32[]{:S(2)}) collective-permute-start(f32[4,1,8,128]{3,2,1,0:T(8,128)S(1)} %get-tuple-element.75), channel_id=1, source_target_pairs={{16,0},{32,16},{48,32},{64,48},{80,64},{96,80},{112,96},{128,112},... | collective-permute-start | bytes 49160 | tf_op jit(solution)/shard_map/ppermute | solution.py:25
  71.8 1.9 collective-permute-start.11
  73.7 3.9 %collective-permute-start.7 = (f32[4,4,8,1]{3,2,1,0:T(8,128)S(1)}, f32[4,4,8,1]{3,2,1,0:T(8,128)S(1)}, u32[]{:S(2)}, u32[]{:S(2)}) collective-permute-start(f32[4,4,8,1]{3,2,1,0:T(8,128)S(1)} %get-tuple-element.70), channel_id=1, source_target_pairs={{0,1},{1,2},{2,3},{3,0},{4,5},{5,6},{6,7},{7,4},{8,9},{9,10},{10,1... | collective-permute-start | bytes 1544 | tf_op jit(solution)/shard_map/ppermute | solution.py:24
  83.5 4.3 %collective-permute-start.12 = (f32[4,4,8,1]{3,2,1,0:T(8,128)S(1)}, f32[4,4,8,1]{3,2,1,0:T(8,128)S(1)}, u32[]{:S(2)}, u32[]{:S(2)}) collective-permute-start(f32[4,4,8,1]{3,2,1,0:T(8,128)S(1)} %get-tuple-element.59), channel_id=1, source_target_pairs={{1,0},{2,1},{3,2},{0,3},{5,4},{6,5},{7,6},{4,7},{9,8},{10,9},{11,1... | collective-permute-start | bytes 1544 | tf_op jit(solution)/shard_map/ppermute | solution.py:25
  87.8 4.8 %collective-permute-start.14 = (f32[4,4,1,128]{3,2,1,0:T(1,128)S(1)}, f32[4,4,1,128]{3,2,1,0:T(1,128)S(1)}, u32[]{:S(2)}, u32[]{:S(2)}) collective-permute-start(f32[4,4,1,128]{3,2,1,0:T(1,128)S(1)} %get-tuple-element.63), channel_id=1, source_target_pairs={{4,0},{8,4},{12,8},{0,12},{5,1},{9,5},{13,9},{1,13},{6,2},{10,6},{... | collective-permute-start | bytes 24584 | tf_op jit(solution)/shard_map/ppermute | solution.py:25
  94.6 5.8 %collective-permute-start.16 = (f32[4,1,8,128]{3,2,1,0:T(8,128)S(1)}, f32[4,1,8,128]{3,2,1,0:T(8,128)S(1)}, u32[]{:S(2)}, u32[]{:S(2)}) collective-permute-start(f32[4,1,8,128]{3,2,1,0:T(8,128)S(1)} %get-tuple-element.65), channel_id=1, source_target_pairs={{16,0},{32,16},{48,32},{64,48},{80,64},{96,80},{112,96},{128,112},... | collective-permute-start | bytes 49160 | tf_op jit(solution)/shard_map/ppermute | solution.py:25
  102.3 3.9 %collective-permute-start.13 = (f32[4,4,8,1]{3,2,1,0:T(8,128)S(1)}, f32[4,4,8,1]{3,2,1,0:T(8,128)S(1)}, u32[]{:S(2)}, u32[]{:S(2)}) collective-permute-start(f32[4,4,8,1]{3,2,1,0:T(8,128)S(1)} %get-tuple-element.60), channel_id=1, source_target_pairs={{0,1},{1,2},{2,3},{3,0},{4,5},{5,6},{6,7},{7,4},{8,9},{9,10},{10,1... | collective-permute-start | bytes 1544 | tf_op jit(solution)/shard_map/ppermute | solution.py:24
  111.7 4.3 %collective-permute-start.18 = (f32[4,4,8,1]{3,2,1,0:T(8,128)S(1)}, f32[4,4,8,1]{3,2,1,0:T(8,128)S(1)}, u32[]{:S(2)}, u32[]{:S(2)}) collective-permute-start(f32[4,4,8,1]{3,2,1,0:T(8,128)S(1)} %get-tuple-element.49), channel_id=1, source_target_pairs={{1,0},{2,1},{3,2},{0,3},{5,4},{6,5},{7,6},{4,7},{9,8},{10,9},{11,1... | collective-permute-start | bytes 1544 | tf_op jit(solution)/shard_map/ppermute | solution.py:25
  116.0 4.9 %collective-permute-start.20 = (f32[4,4,1,128]{3,2,1,0:T(1,128)S(1)}, f32[4,4,1,128]{3,2,1,0:T(1,128)S(1)}, u32[]{:S(2)}, u32[]{:S(2)}) collective-permute-start(f32[4,4,1,128]{3,2,1,0:T(1,128)S(1)} %get-tuple-element.53), channel_id=1, source_target_pairs={{4,0},{8,4},{12,8},{0,12},{5,1},{9,5},{13,9},{1,13},{6,2},{10,6},{... | collective-permute-start | bytes 24584 | tf_op jit(solution)/shard_map/ppermute | solution.py:25
  122.8 5.8 %collective-permute-start.22 = (f32[4,1,8,128]{3,2,1,0:T(8,128)S(1)}, f32[4,1,8,128]{3,2,1,0:T(8,128)S(1)}, u32[]{:S(2)}, u32[]{:S(2)}) collective-permute-start(f32[4,1,8,128]{3,2,1,0:T(8,128)S(1)} %get-tuple-element.55), channel_id=1, source_target_pairs={{16,0},{32,16},{48,32},{64,48},{80,64},{96,80},{112,96},{128,112},... | collective-permute-start | bytes 49160 | tf_op jit(solution)/shard_map/ppermute | solution.py:25
  130.5 3.9 %collective-permute-start.19 = (f32[4,4,8,1]{3,2,1,0:T(8,128)S(1)}, f32[4,4,8,1]{3,2,1,0:T(8,128)S(1)}, u32[]{:S(2)}, u32[]{:S(2)}) collective-permute-start(f32[4,4,8,1]{3,2,1,0:T(8,128)S(1)} %get-tuple-element.50), channel_id=1, source_target_pairs={{0,1},{1,2},{2,3},{3,0},{4,5},{5,6},{6,7},{7,4},{8,9},{9,10},{10,1... | collective-permute-start | bytes 1544 | tf_op jit(solution)/shard_map/ppermute | solution.py:24
  140.1 4.8 %collective-permute-start.26 = (f32[2,4,1,128]{3,2,1,0:T(1,128)}, f32[2,4,1,128]{3,2,1,0:T(1,128)}, u32[]{:S(2)}, u32[]{:S(2)}) collective-permute-start(f32[2,4,1,128]{3,2,1,0:T(1,128)} %get-tuple-element.129), channel_id=1, source_target_pairs={{4,0},{8,4},{12,8},{0,12},{5,1},{9,5},{13,9},{1,13},{6,2},{10,6},{... | collective-permute-start | bytes 12296 | tf_op jit(solution)/shard_map/ppermute | solution.py:25
  144.9 1.9 collective-permute-start.27
  147.5 5.1 %collective-permute-start.28 = (f32[2,1,8,128]{3,2,1,0:T(8,128)}, f32[2,1,8,128]{3,2,1,0:T(8,128)}, u32[]{:S(2)}, u32[]{:S(2)}) collective-permute-start(f32[2,1,8,128]{3,2,1,0:T(8,128)} %get-tuple-element.133), channel_id=1, source_target_pairs={{16,0},{32,16},{48,32},{64,48},{80,64},{96,80},{112,96},{128,112},... | collective-permute-start | bytes 24584 | tf_op jit(solution)/shard_map/ppermute | solution.py:25
  152.6 5.5 %collective-permute-start.24 = (f32[2,4,8,1]{3,2,1,0:T(8,128)}, f32[2,4,8,1]{3,2,1,0:T(8,128)}, u32[]{:S(2)}, u32[]{:S(2)}) collective-permute-start(f32[2,4,8,1]{3,2,1,0:T(8,128)} %get-tuple-element.125), channel_id=1, source_target_pairs={{1,0},{2,1},{3,2},{0,3},{5,4},{6,5},{7,6},{4,7},{9,8},{10,9},{11,1... | collective-permute-start | bytes 776 | tf_op jit(solution)/shard_map/ppermute | solution.py:25
  158.1 3.4 collective-permute-start.25
  165.2 3.7 collective-permute-done.29
  173.7 2.1 fusion.34
  181.7 4.8 %collective-permute-start.32 = (f32[2,4,1,128]{3,2,1,0:T(1,128)S(1)}, f32[2,4,1,128]{3,2,1,0:T(1,128)S(1)}, u32[]{:S(2)}, u32[]{:S(2)}) collective-permute-start(f32[2,4,1,128]{3,2,1,0:T(1,128)S(1)} %get-tuple-element.117), channel_id=1, source_target_pairs={{4,0},{8,4},{12,8},{0,12},{5,1},{9,5},{13,9},{1,13},{6,2},{10,6},{... | collective-permute-start | bytes 12296 | tf_op jit(solution)/shard_map/ppermute | solution.py:25
  188.5 2.4 collective-permute-start.30
  190.9 4.7 %collective-permute-start.31 = (f32[2,4,8,1]{3,2,1,0:T(8,128)S(1)}, f32[2,4,8,1]{3,2,1,0:T(8,128)S(1)}, u32[]{:S(2)}, u32[]{:S(2)}) collective-permute-start(f32[2,4,8,1]{3,2,1,0:T(8,128)S(1)} %get-tuple-element.114), channel_id=1, source_target_pairs={{0,1},{1,2},{2,3},{3,0},{4,5},{5,6},{6,7},{7,4},{8,9},{9,10},{10,1... | collective-permute-start | bytes 776 | tf_op jit(solution)/shard_map/ppermute | solution.py:24
  195.6 1.9 collective-permute-start.34
  197.6 3.5 collective-permute-start.35
  201.4 2.7 collective-permute-done.35
  208.5 2.2 convert_reduce_fusion.2
  216.0 4.6 %collective-permute-start.38 = (f32[2,4,1,128]{3,2,1,0:T(1,128)S(1)}, f32[2,4,1,128]{3,2,1,0:T(1,128)S(1)}, u32[]{:S(2)}, u32[]{:S(2)}) collective-permute-start(f32[2,4,1,128]{3,2,1,0:T(1,128)S(1)} %get-tuple-element.105), channel_id=1, source_target_pairs={{4,0},{8,4},{12,8},{0,12},{5,1},{9,5},{13,9},{1,13},{6,2},{10,6},{... | collective-permute-start | bytes 12296 | tf_op jit(solution)/shard_map/ppermute | solution.py:25
  224.4 5.1 %collective-permute-start.37 = (f32[2,4,8,1]{3,2,1,0:T(8,128)S(1)}, f32[2,4,8,1]{3,2,1,0:T(8,128)S(1)}, u32[]{:S(2)}, u32[]{:S(2)}) collective-permute-start(f32[2,4,8,1]{3,2,1,0:T(8,128)S(1)} %get-tuple-element.102), channel_id=1, source_target_pairs={{0,1},{1,2},{2,3},{3,0},{4,5},{5,6},{6,7},{7,4},{8,9},{9,10},{10,1... | collective-permute-start | bytes 776 | tf_op jit(solution)/shard_map/ppermute | solution.py:24
  229.6 1.9 collective-permute-start.40
  231.5 3.4 collective-permute-start.41
  235.2 2.8 collective-permute-done.41
  242.4 2.2 convert_reduce_fusion.1
  249.8 4.6 %collective-permute-start.44 = (f32[2,4,1,128]{3,2,1,0:T(1,128)S(1)}, f32[2,4,1,128]{3,2,1,0:T(1,128)S(1)}, u32[]{:S(2)}, u32[]{:S(2)}) collective-permute-start(f32[2,4,1,128]{3,2,1,0:T(1,128)S(1)} %get-tuple-element.93), channel_id=1, source_target_pairs={{4,0},{8,4},{12,8},{0,12},{5,1},{9,5},{13,9},{1,13},{6,2},{10,6},{... | collective-permute-start | bytes 12296 | tf_op jit(solution)/shard_map/ppermute | solution.py:25
  256.3 2.2 collective-permute-start.42
  258.5 4.8 %collective-permute-start.43 = (f32[2,4,8,1]{3,2,1,0:T(8,128)S(1)}, f32[2,4,8,1]{3,2,1,0:T(8,128)S(1)}, u32[]{:S(2)}, u32[]{:S(2)}) collective-permute-start(f32[2,4,8,1]{3,2,1,0:T(8,128)S(1)} %get-tuple-element.90), channel_id=1, source_target_pairs={{0,1},{1,2},{2,3},{3,0},{4,5},{5,6},{6,7},{7,4},{8,9},{9,10},{10,1... | collective-permute-start | bytes 776 | tf_op jit(solution)/shard_map/ppermute | solution.py:24
  263.3 1.9 collective-permute-start.46
  265.3 3.4 collective-permute-start.47
  269.0 2.8 collective-permute-done.47
  276.9 101.3 %psum.7 = f32[5255]{0:T(1024)S(1)} all-reduce(f32[5255]{0:T(1024)S(1)} %concatenate.436), channel_id=1, replica_groups=mesh['blk'=32,'gy'=4,'rep'=4] {'blk','gy','rep'}, use_global_device_ids=true, to_apply=%region_13.0 | all-reduce | flops 5255 | bytes 42040 | tf_op jit(solution)/shard_map/psum | solution.py:188
  (851 shorter events, 91.9 us)
Async XLA Ops:
  25.0 25.5 %collective-permute-start.2 = (f32[4,4,1,128]{3,2,1,0:T(1,128)S(1)}, f32[4,4,1,128]{3,2,1,0:T(1,128)S(1)}, u32[]{:S(2)}, u32[]{:S(2)}) collective-permute-start(f32[4,4,1,128]{3,2,1,0:T(1,128)S(1)} %get-tuple-element.83), channel_id=1, source_target_pairs={{4,0},{8,4},{12,8},{0,12},{5,1},{9,5},{13,9},{1,13},{6,2},{10,6},{... | collective-permute-start | bytes 24584 | tf_op jit(solution)/shard_map/ppermute | solution.py:25
  26.9 23.6 %collective-permute-start.3 = (f32[4,4,1,128]{3,2,1,0:T(1,128)S(1)}, f32[4,4,1,128]{3,2,1,0:T(1,128)S(1)}, u32[]{:S(2)}, u32[]{:S(2)}) collective-permute-start(f32[4,4,1,128]{3,2,1,0:T(1,128)S(1)} %get-tuple-element.84), channel_id=1, source_target_pairs={{0,4},{4,8},{8,12},{12,0},{1,5},{5,9},{9,13},{13,1},{2,6},{6,10},{... | collective-permute-start | bytes 24584 | tf_op jit(solution)/shard_map/ppermute | solution.py:24
  30.3 20.2 %collective-permute-start.4 = (f32[4,1,8,128]{3,2,1,0:T(8,128)S(1)}, f32[4,1,8,128]{3,2,1,0:T(8,128)S(1)}, u32[]{:S(2)}, u32[]{:S(2)}) collective-permute-start(f32[4,1,8,128]{3,2,1,0:T(8,128)S(1)} %get-tuple-element.85), channel_id=1, source_target_pairs={{16,0},{32,16},{48,32},{64,48},{80,64},{96,80},{112,96},{128,112},... | collective-permute-start | bytes 49160 | tf_op jit(solution)/shard_map/ppermute | solution.py:25
  38.1 12.5 %collective-permute-start.5 = (f32[4,1,8,128]{3,2,1,0:T(8,128)S(1)}, f32[4,1,8,128]{3,2,1,0:T(8,128)S(1)}, u32[]{:S(2)}, u32[]{:S(2)}) collective-permute-start(f32[4,1,8,128]{3,2,1,0:T(8,128)S(1)} %get-tuple-element.86), channel_id=1, source_target_pairs={{0,16},{16,32},{32,48},{48,64},{64,80},{80,96},{96,112},{112,128},... | collective-permute-start | bytes 49160 | tf_op jit(solution)/shard_map/ppermute | solution.py:24
  40.1 7.1 %collective-permute-start = (f32[4,4,8,1]{3,2,1,0:T(8,128)S(1)}, f32[4,4,8,1]{3,2,1,0:T(8,128)S(1)}, u32[]{:S(2)}, u32[]{:S(2)}) collective-permute-start(f32[4,4,8,1]{3,2,1,0:T(8,128)S(1)} %get-tuple-element.79), channel_id=1, source_target_pairs={{1,0},{2,1},{3,2},{0,3},{5,4},{6,5},{7,6},{4,7},{9,8},{10,9},{11,1... | collective-permute-start | bytes 1544 | tf_op jit(solution)/shard_map/ppermute | solution.py:25
  47.2 3.2 collective-permute-start.1
  54.9 18.8 %collective-permute-start.6 = (f32[4,4,8,1]{3,2,1,0:T(8,128)S(1)}, f32[4,4,8,1]{3,2,1,0:T(8,128)S(1)}, u32[]{:S(2)}, u32[]{:S(2)}) collective-permute-start(f32[4,4,8,1]{3,2,1,0:T(8,128)S(1)} %get-tuple-element.69), channel_id=1, source_target_pairs={{1,0},{2,1},{3,2},{0,3},{5,4},{6,5},{7,6},{4,7},{9,8},{10,9},{11,1... | collective-permute-start | bytes 1544 | tf_op jit(solution)/shard_map/ppermute | solution.py:25
  60.4 18.6 %collective-permute-start.8 = (f32[4,4,1,128]{3,2,1,0:T(1,128)S(1)}, f32[4,4,1,128]{3,2,1,0:T(1,128)S(1)}, u32[]{:S(2)}, u32[]{:S(2)}) collective-permute-start(f32[4,4,1,128]{3,2,1,0:T(1,128)S(1)} %get-tuple-element.73), channel_id=1, source_target_pairs={{4,0},{8,4},{12,8},{0,12},{5,1},{9,5},{13,9},{1,13},{6,2},{10,6},{... | collective-permute-start | bytes 24584 | tf_op jit(solution)/shard_map/ppermute | solution.py:25
  65.0 14.1 %collective-permute-start.9 = (f32[4,4,1,128]{3,2,1,0:T(1,128)S(1)}, f32[4,4,1,128]{3,2,1,0:T(1,128)S(1)}, u32[]{:S(2)}, u32[]{:S(2)}) collective-permute-start(f32[4,4,1,128]{3,2,1,0:T(1,128)S(1)} %get-tuple-element.74), channel_id=1, source_target_pairs={{0,4},{4,8},{8,12},{12,0},{1,5},{5,9},{9,13},{13,1},{2,6},{6,10},{... | collective-permute-start | bytes 24584 | tf_op jit(solution)/shard_map/ppermute | solution.py:24
  66.9 12.2 %collective-permute-start.10 = (f32[4,1,8,128]{3,2,1,0:T(8,128)S(1)}, f32[4,1,8,128]{3,2,1,0:T(8,128)S(1)}, u32[]{:S(2)}, u32[]{:S(2)}) collective-permute-start(f32[4,1,8,128]{3,2,1,0:T(8,128)S(1)} %get-tuple-element.75), channel_id=1, source_target_pairs={{16,0},{32,16},{48,32},{64,48},{80,64},{96,80},{112,96},{128,112},... | collective-permute-start | bytes 49160 | tf_op jit(solution)/shard_map/ppermute | solution.py:25
  71.8 7.4 %collective-permute-start.11 = (f32[4,1,8,128]{3,2,1,0:T(8,128)S(1)}, f32[4,1,8,128]{3,2,1,0:T(8,128)S(1)}, u32[]{:S(2)}, u32[]{:S(2)}) collective-permute-start(f32[4,1,8,128]{3,2,1,0:T(8,128)S(1)} %get-tuple-element.76), channel_id=1, source_target_pairs={{0,16},{16,32},{32,48},{48,64},{64,80},{80,96},{96,112},{112,128},... | collective-permute-start | bytes 49160 | tf_op jit(solution)/shard_map/ppermute | solution.py:24
  73.7 5.3 %collective-permute-start.7 = (f32[4,4,8,1]{3,2,1,0:T(8,128)S(1)}, f32[4,4,8,1]{3,2,1,0:T(8,128)S(1)}, u32[]{:S(2)}, u32[]{:S(2)}) collective-permute-start(f32[4,4,8,1]{3,2,1,0:T(8,128)S(1)} %get-tuple-element.70), channel_id=1, source_target_pairs={{0,1},{1,2},{2,3},{3,0},{4,5},{5,6},{6,7},{7,4},{8,9},{9,10},{10,1... | collective-permute-start | bytes 1544 | tf_op jit(solution)/shard_map/ppermute | solution.py:24
  83.5 18.8 %collective-permute-start.12 = (f32[4,4,8,1]{3,2,1,0:T(8,128)S(1)}, f32[4,4,8,1]{3,2,1,0:T(8,128)S(1)}, u32[]{:S(2)}, u32[]{:S(2)}) collective-permute-start(f32[4,4,8,1]{3,2,1,0:T(8,128)S(1)} %get-tuple-element.59), channel_id=1, source_target_pairs={{1,0},{2,1},{3,2},{0,3},{5,4},{6,5},{7,6},{4,7},{9,8},{10,9},{11,1... | collective-permute-start | bytes 1544 | tf_op jit(solution)/shard_map/ppermute | solution.py:25
  87.8 19.8 %collective-permute-start.14 = (f32[4,4,1,128]{3,2,1,0:T(1,128)S(1)}, f32[4,4,1,128]{3,2,1,0:T(1,128)S(1)}, u32[]{:S(2)}, u32[]{:S(2)}) collective-permute-start(f32[4,4,1,128]{3,2,1,0:T(1,128)S(1)} %get-tuple-element.63), channel_id=1, source_target_pairs={{4,0},{8,4},{12,8},{0,12},{5,1},{9,5},{13,9},{1,13},{6,2},{10,6},{... | collective-permute-start | bytes 24584 | tf_op jit(solution)/shard_map/ppermute | solution.py:25
  92.6 15.0 %collective-permute-start.15 = (f32[4,4,1,128]{3,2,1,0:T(1,128)S(1)}, f32[4,4,1,128]{3,2,1,0:T(1,128)S(1)}, u32[]{:S(2)}, u32[]{:S(2)}) collective-permute-start(f32[4,4,1,128]{3,2,1,0:T(1,128)S(1)} %get-tuple-element.64), channel_id=1, source_target_pairs={{0,4},{4,8},{8,12},{12,0},{1,5},{5,9},{9,13},{13,1},{2,6},{6,10},{... | collective-permute-start | bytes 24584 | tf_op jit(solution)/shard_map/ppermute | solution.py:24
  94.6 13.1 %collective-permute-start.16 = (f32[4,1,8,128]{3,2,1,0:T(8,128)S(1)}, f32[4,1,8,128]{3,2,1,0:T(8,128)S(1)}, u32[]{:S(2)}, u32[]{:S(2)}) collective-permute-start(f32[4,1,8,128]{3,2,1,0:T(8,128)S(1)} %get-tuple-element.65), channel_id=1, source_target_pairs={{16,0},{32,16},{48,32},{64,48},{80,64},{96,80},{112,96},{128,112},... | collective-permute-start | bytes 49160 | tf_op jit(solution)/shard_map/ppermute | solution.py:25
  100.3 7.4 %collective-permute-start.17 = (f32[4,1,8,128]{3,2,1,0:T(8,128)S(1)}, f32[4,1,8,128]{3,2,1,0:T(8,128)S(1)}, u32[]{:S(2)}, u32[]{:S(2)}) collective-permute-start(f32[4,1,8,128]{3,2,1,0:T(8,128)S(1)} %get-tuple-element.66), channel_id=1, source_target_pairs={{0,16},{16,32},{32,48},{48,64},{64,80},{80,96},{96,112},{112,128},... | collective-permute-start | bytes 49160 | tf_op jit(solution)/shard_map/ppermute | solution.py:24
  102.3 5.3 %collective-permute-start.13 = (f32[4,4,8,1]{3,2,1,0:T(8,128)S(1)}, f32[4,4,8,1]{3,2,1,0:T(8,128)S(1)}, u32[]{:S(2)}, u32[]{:S(2)}) collective-permute-start(f32[4,4,8,1]{3,2,1,0:T(8,128)S(1)} %get-tuple-element.60), channel_id=1, source_target_pairs={{0,1},{1,2},{2,3},{3,0},{4,5},{5,6},{6,7},{7,4},{8,9},{9,10},{10,1... | collective-permute-start | bytes 1544 | tf_op jit(solution)/shard_map/ppermute | solution.py:24
  111.7 18.8 %collective-permute-start.18 = (f32[4,4,8,1]{3,2,1,0:T(8,128)S(1)}, f32[4,4,8,1]{3,2,1,0:T(8,128)S(1)}, u32[]{:S(2)}, u32[]{:S(2)}) collective-permute-start(f32[4,4,8,1]{3,2,1,0:T(8,128)S(1)} %get-tuple-element.49), channel_id=1, source_target_pairs={{1,0},{2,1},{3,2},{0,3},{5,4},{6,5},{7,6},{4,7},{9,8},{10,9},{11,1... | collective-permute-start | bytes 1544 | tf_op jit(solution)/shard_map/ppermute | solution.py:25
  116.0 19.8 %collective-permute-start.20 = (f32[4,4,1,128]{3,2,1,0:T(1,128)S(1)}, f32[4,4,1,128]{3,2,1,0:T(1,128)S(1)}, u32[]{:S(2)}, u32[]{:S(2)}) collective-permute-start(f32[4,4,1,128]{3,2,1,0:T(1,128)S(1)} %get-tuple-element.53), channel_id=1, source_target_pairs={{4,0},{8,4},{12,8},{0,12},{5,1},{9,5},{13,9},{1,13},{6,2},{10,6},{... | collective-permute-start | bytes 24584 | tf_op jit(solution)/shard_map/ppermute | solution.py:25
  120.9 15.0 %collective-permute-start.21 = (f32[4,4,1,128]{3,2,1,0:T(1,128)S(1)}, f32[4,4,1,128]{3,2,1,0:T(1,128)S(1)}, u32[]{:S(2)}, u32[]{:S(2)}) collective-permute-start(f32[4,4,1,128]{3,2,1,0:T(1,128)S(1)} %get-tuple-element.54), channel_id=1, source_target_pairs={{0,4},{4,8},{8,12},{12,0},{1,5},{5,9},{9,13},{13,1},{2,6},{6,10},{... | collective-permute-start | bytes 24584 | tf_op jit(solution)/shard_map/ppermute | solution.py:24
  122.8 13.1 %collective-permute-start.22 = (f32[4,1,8,128]{3,2,1,0:T(8,128)S(1)}, f32[4,1,8,128]{3,2,1,0:T(8,128)S(1)}, u32[]{:S(2)}, u32[]{:S(2)}) collective-permute-start(f32[4,1,8,128]{3,2,1,0:T(8,128)S(1)} %get-tuple-element.55), channel_id=1, source_target_pairs={{16,0},{32,16},{48,32},{64,48},{80,64},{96,80},{112,96},{128,112},... | collective-permute-start | bytes 49160 | tf_op jit(solution)/shard_map/ppermute | solution.py:25
  128.5 7.4 %collective-permute-start.23 = (f32[4,1,8,128]{3,2,1,0:T(8,128)S(1)}, f32[4,1,8,128]{3,2,1,0:T(8,128)S(1)}, u32[]{:S(2)}, u32[]{:S(2)}) collective-permute-start(f32[4,1,8,128]{3,2,1,0:T(8,128)S(1)} %get-tuple-element.56), channel_id=1, source_target_pairs={{0,16},{16,32},{32,48},{48,64},{64,80},{80,96},{96,112},{112,128},... | collective-permute-start | bytes 49160 | tf_op jit(solution)/shard_map/ppermute | solution.py:24
  130.5 5.3 %collective-permute-start.19 = (f32[4,4,8,1]{3,2,1,0:T(8,128)S(1)}, f32[4,4,8,1]{3,2,1,0:T(8,128)S(1)}, u32[]{:S(2)}, u32[]{:S(2)}) collective-permute-start(f32[4,4,8,1]{3,2,1,0:T(8,128)S(1)} %get-tuple-element.50), channel_id=1, source_target_pairs={{0,1},{1,2},{2,3},{3,0},{4,5},{5,6},{6,7},{7,4},{8,9},{9,10},{10,1... | collective-permute-start | bytes 1544 | tf_op jit(solution)/shard_map/ppermute | solution.py:24
  140.1 24.1 %collective-permute-start.26 = (f32[2,4,1,128]{3,2,1,0:T(1,128)}, f32[2,4,1,128]{3,2,1,0:T(1,128)}, u32[]{:S(2)}, u32[]{:S(2)}) collective-permute-start(f32[2,4,1,128]{3,2,1,0:T(1,128)} %get-tuple-element.129), channel_id=1, source_target_pairs={{4,0},{8,4},{12,8},{0,12},{5,1},{9,5},{13,9},{1,13},{6,2},{10,6},{... | collective-permute-start | bytes 12296 | tf_op jit(solution)/shard_map/ppermute | solution.py:25
  144.9 19.2 %collective-permute-start.27 = (f32[2,4,1,128]{3,2,1,0:T(1,128)}, f32[2,4,1,128]{3,2,1,0:T(1,128)}, u32[]{:S(2)}, u32[]{:S(2)}) collective-permute-start(f32[2,4,1,128]{3,2,1,0:T(1,128)} %get-tuple-element.130), channel_id=1, source_target_pairs={{0,4},{4,8},{8,12},{12,0},{1,5},{5,9},{9,13},{13,1},{2,6},{6,10},{... | collective-permute-start | bytes 12296 | tf_op jit(solution)/shard_map/ppermute | solution.py:24
  147.5 17.7 %collective-permute-start.28 = (f32[2,1,8,128]{3,2,1,0:T(8,128)}, f32[2,1,8,128]{3,2,1,0:T(8,128)}, u32[]{:S(2)}, u32[]{:S(2)}) collective-permute-start(f32[2,1,8,128]{3,2,1,0:T(8,128)} %get-tuple-element.133), channel_id=1, source_target_pairs={{16,0},{32,16},{48,32},{64,48},{80,64},{96,80},{112,96},{128,112},... | collective-permute-start | bytes 24584 | tf_op jit(solution)/shard_map/ppermute | solution.py:25
  152.6 9.6 %collective-permute-start.24 = (f32[2,4,8,1]{3,2,1,0:T(8,128)}, f32[2,4,8,1]{3,2,1,0:T(8,128)}, u32[]{:S(2)}, u32[]{:S(2)}) collective-permute-start(f32[2,4,8,1]{3,2,1,0:T(8,128)} %get-tuple-element.125), channel_id=1, source_target_pairs={{1,0},{2,1},{3,2},{0,3},{5,4},{6,5},{7,6},{4,7},{9,8},{10,9},{11,1... | collective-permute-start | bytes 776 | tf_op jit(solution)/shard_map/ppermute | solution.py:25
  158.1 6.0 %collective-permute-start.25 = (f32[2,4,8,1]{3,2,1,0:T(8,128)}, f32[2,4,8,1]{3,2,1,0:T(8,128)}, u32[]{:S(2)}, u32[]{:S(2)}) collective-permute-start(f32[2,4,8,1]{3,2,1,0:T(8,128)} %get-tuple-element.126), channel_id=1, source_target_pairs={{0,1},{1,2},{2,3},{3,0},{4,5},{5,6},{6,7},{7,4},{8,9},{9,10},{10,1... | collective-permute-start | bytes 776 | tf_op jit(solution)/shard_map/ppermute | solution.py:24
  162.2 6.7 %collective-permute-start.29 = (f32[2,1,8,128]{3,2,1,0:T(8,128)}, f32[2,1,8,128]{3,2,1,0:T(8,128)S(1)}, u32[]{:S(2)}, u32[]{:S(2)}) collective-permute-start(f32[2,1,8,128]{3,2,1,0:T(8,128)} %get-tuple-element.134), channel_id=1, source_target_pairs={{0,16},{16,32},{32,48},{48,64},{64,80},{80,96},{96,112},{112,128},... | collective-permute-start | bytes 24584 | tf_op jit(solution)/shard_map/ppermute | solution.py:24
  181.7 19.4 %collective-permute-start.32 = (f32[2,4,1,128]{3,2,1,0:T(1,128)S(1)}, f32[2,4,1,128]{3,2,1,0:T(1,128)S(1)}, u32[]{:S(2)}, u32[]{:S(2)}) collective-permute-start(f32[2,4,1,128]{3,2,1,0:T(1,128)S(1)} %get-tuple-element.117), channel_id=1, source_target_pairs={{4,0},{8,4},{12,8},{0,12},{5,1},{9,5},{13,9},{1,13},{6,2},{10,6},{... | collective-permute-start | bytes 12296 | tf_op jit(solution)/shard_map/ppermute | solution.py:25
  186.6 14.6 %collective-permute-start.33 = (f32[2,4,1,128]{3,2,1,0:T(1,128)S(1)}, f32[2,4,1,128]{3,2,1,0:T(1,128)S(1)}, u32[]{:S(2)}, u32[]{:S(2)}) collective-permute-start(f32[2,4,1,128]{3,2,1,0:T(1,128)S(1)} %get-tuple-element.118), channel_id=1, source_target_pairs={{0,4},{4,8},{8,12},{12,0},{1,5},{5,9},{9,13},{13,1},{2,6},{6,10},{... | collective-permute-start | bytes 12296 | tf_op jit(solution)/shard_map/ppermute | solution.py:24
  188.5 9.0 %collective-permute-start.30 = (f32[2,4,8,1]{3,2,1,0:T(8,128)S(1)}, f32[2,4,8,1]{3,2,1,0:T(8,128)S(1)}, u32[]{:S(2)}, u32[]{:S(2)}) collective-permute-start(f32[2,4,8,1]{3,2,1,0:T(8,128)S(1)} %get-tuple-element.113), channel_id=1, source_target_pairs={{1,0},{2,1},{3,2},{0,3},{5,4},{6,5},{7,6},{4,7},{9,8},{10,9},{11,1... | collective-permute-start | bytes 776 | tf_op jit(solution)/shard_map/ppermute | solution.py:25
  190.9 10.2 %collective-permute-start.31 = (f32[2,4,8,1]{3,2,1,0:T(8,128)S(1)}, f32[2,4,8,1]{3,2,1,0:T(8,128)S(1)}, u32[]{:S(2)}, u32[]{:S(2)}) collective-permute-start(f32[2,4,8,1]{3,2,1,0:T(8,128)S(1)} %get-tuple-element.114), channel_id=1, source_target_pairs={{0,1},{1,2},{2,3},{3,0},{4,5},{5,6},{6,7},{7,4},{8,9},{9,10},{10,1... | collective-permute-start | bytes 776 | tf_op jit(solution)/shard_map/ppermute | solution.py:24
  195.6 5.8 %collective-permute-start.34 = (f32[2,1,8,128]{3,2,1,0:T(8,128)S(1)}, f32[2,1,8,128]{3,2,1,0:T(8,128)S(1)}, u32[]{:S(2)}, u32[]{:S(2)}) collective-permute-start(f32[2,1,8,128]{3,2,1,0:T(8,128)S(1)} %get-tuple-element.121), channel_id=1, source_target_pairs={{16,0},{32,16},{48,32},{64,48},{80,64},{96,80},{112,96},{128,112},... | collective-permute-start | bytes 24584 | tf_op jit(solution)/shard_map/ppermute | solution.py:25
  197.6 6.5 %collective-permute-start.35 = (f32[2,1,8,128]{3,2,1,0:T(8,128)S(1)}, f32[2,1,8,128]{3,2,1,0:T(8,128)S(1)}, u32[]{:S(2)}, u32[]{:S(2)}) collective-permute-start(f32[2,1,8,128]{3,2,1,0:T(8,128)S(1)} %get-tuple-element.122), channel_id=1, source_target_pairs={{0,16},{16,32},{32,48},{48,64},{64,80},{80,96},{96,112},{112,128},... | collective-permute-start | bytes 24584 | tf_op jit(solution)/shard_map/ppermute | solution.py:24
  216.0 18.9 %collective-permute-start.38 = (f32[2,4,1,128]{3,2,1,0:T(1,128)S(1)}, f32[2,4,1,128]{3,2,1,0:T(1,128)S(1)}, u32[]{:S(2)}, u32[]{:S(2)}) collective-permute-start(f32[2,4,1,128]{3,2,1,0:T(1,128)S(1)} %get-tuple-element.105), channel_id=1, source_target_pairs={{4,0},{8,4},{12,8},{0,12},{5,1},{9,5},{13,9},{1,13},{6,2},{10,6},{... | collective-permute-start | bytes 12296 | tf_op jit(solution)/shard_map/ppermute | solution.py:25
  220.5 14.4 %collective-permute-start.39 = (f32[2,4,1,128]{3,2,1,0:T(1,128)S(1)}, f32[2,4,1,128]{3,2,1,0:T(1,128)S(1)}, u32[]{:S(2)}, u32[]{:S(2)}) collective-permute-start(f32[2,4,1,128]{3,2,1,0:T(1,128)S(1)} %get-tuple-element.106), channel_id=1, source_target_pairs={{0,4},{4,8},{8,12},{12,0},{1,5},{5,9},{9,13},{13,1},{2,6},{6,10},{... | collective-permute-start | bytes 12296 | tf_op jit(solution)/shard_map/ppermute | solution.py:24
  222.5 9.0 %collective-permute-start.36 = (f32[2,4,8,1]{3,2,1,0:T(8,128)S(1)}, f32[2,4,8,1]{3,2,1,0:T(8,128)S(1)}, u32[]{:S(2)}, u32[]{:S(2)}) collective-permute-start(f32[2,4,8,1]{3,2,1,0:T(8,128)S(1)} %get-tuple-element.101), channel_id=1, source_target_pairs={{1,0},{2,1},{3,2},{0,3},{5,4},{6,5},{7,6},{4,7},{9,8},{10,9},{11,1... | collective-permute-start | bytes 776 | tf_op jit(solution)/shard_map/ppermute | solution.py:25
  224.4 10.5 %collective-permute-start.37 = (f32[2,4,8,1]{3,2,1,0:T(8,128)S(1)}, f32[2,4,8,1]{3,2,1,0:T(8,128)S(1)}, u32[]{:S(2)}, u32[]{:S(2)}) collective-permute-start(f32[2,4,8,1]{3,2,1,0:T(8,128)S(1)} %get-tuple-element.102), channel_id=1, source_target_pairs={{0,1},{1,2},{2,3},{3,0},{4,5},{5,6},{6,7},{7,4},{8,9},{9,10},{10,1... | collective-permute-start | bytes 776 | tf_op jit(solution)/shard_map/ppermute | solution.py:24
  229.6 5.6 %collective-permute-start.40 = (f32[2,1,8,128]{3,2,1,0:T(8,128)S(1)}, f32[2,1,8,128]{3,2,1,0:T(8,128)S(1)}, u32[]{:S(2)}, u32[]{:S(2)}) collective-permute-start(f32[2,1,8,128]{3,2,1,0:T(8,128)S(1)} %get-tuple-element.109), channel_id=1, source_target_pairs={{16,0},{32,16},{48,32},{64,48},{80,64},{96,80},{112,96},{128,112},... | collective-permute-start | bytes 24584 | tf_op jit(solution)/shard_map/ppermute | solution.py:25
  231.5 6.5 %collective-permute-start.41 = (f32[2,1,8,128]{3,2,1,0:T(8,128)S(1)}, f32[2,1,8,128]{3,2,1,0:T(8,128)S(1)}, u32[]{:S(2)}, u32[]{:S(2)}) collective-permute-start(f32[2,1,8,128]{3,2,1,0:T(8,128)S(1)} %get-tuple-element.110), channel_id=1, source_target_pairs={{0,16},{16,32},{32,48},{48,64},{64,80},{80,96},{96,112},{112,128},... | collective-permute-start | bytes 24584 | tf_op jit(solution)/shard_map/ppermute | solution.py:24
  249.8 18.9 %collective-permute-start.44 = (f32[2,4,1,128]{3,2,1,0:T(1,128)S(1)}, f32[2,4,1,128]{3,2,1,0:T(1,128)S(1)}, u32[]{:S(2)}, u32[]{:S(2)}) collective-permute-start(f32[2,4,1,128]{3,2,1,0:T(1,128)S(1)} %get-tuple-element.93), channel_id=1, source_target_pairs={{4,0},{8,4},{12,8},{0,12},{5,1},{9,5},{13,9},{1,13},{6,2},{10,6},{... | collective-permute-start | bytes 12296 | tf_op jit(solution)/shard_map/ppermute | solution.py:25
  254.3 14.4 %collective-permute-start.45 = (f32[2,4,1,128]{3,2,1,0:T(1,128)S(1)}, f32[2,4,1,128]{3,2,1,0:T(1,128)S(1)}, u32[]{:S(2)}, u32[]{:S(2)}) collective-permute-start(f32[2,4,1,128]{3,2,1,0:T(1,128)S(1)} %get-tuple-element.94), channel_id=1, source_target_pairs={{0,4},{4,8},{8,12},{12,0},{1,5},{5,9},{9,13},{13,1},{2,6},{6,10},{... | collective-permute-start | bytes 12296 | tf_op jit(solution)/shard_map/ppermute | solution.py:24
  256.3 9.0 %collective-permute-start.42 = (f32[2,4,8,1]{3,2,1,0:T(8,128)S(1)}, f32[2,4,8,1]{3,2,1,0:T(8,128)S(1)}, u32[]{:S(2)}, u32[]{:S(2)}) collective-permute-start(f32[2,4,8,1]{3,2,1,0:T(8,128)S(1)} %get-tuple-element.89), channel_id=1, source_target_pairs={{1,0},{2,1},{3,2},{0,3},{5,4},{6,5},{7,6},{4,7},{9,8},{10,9},{11,1... | collective-permute-start | bytes 776 | tf_op jit(solution)/shard_map/ppermute | solution.py:25
  258.5 10.2 %collective-permute-start.43 = (f32[2,4,8,1]{3,2,1,0:T(8,128)S(1)}, f32[2,4,8,1]{3,2,1,0:T(8,128)S(1)}, u32[]{:S(2)}, u32[]{:S(2)}) collective-permute-start(f32[2,4,8,1]{3,2,1,0:T(8,128)S(1)} %get-tuple-element.90), channel_id=1, source_target_pairs={{0,1},{1,2},{2,3},{3,0},{4,5},{5,6},{6,7},{7,4},{8,9},{9,10},{10,1... | collective-permute-start | bytes 776 | tf_op jit(solution)/shard_map/ppermute | solution.py:24
  263.3 5.6 %collective-permute-start.46 = (f32[2,1,8,128]{3,2,1,0:T(8,128)S(1)}, f32[2,1,8,128]{3,2,1,0:T(8,128)S(1)}, u32[]{:S(2)}, u32[]{:S(2)}) collective-permute-start(f32[2,1,8,128]{3,2,1,0:T(8,128)S(1)} %get-tuple-element.97), channel_id=1, source_target_pairs={{16,0},{32,16},{48,32},{64,48},{80,64},{96,80},{112,96},{128,112},... | collective-permute-start | bytes 24584 | tf_op jit(solution)/shard_map/ppermute | solution.py:25
  265.3 6.5 %collective-permute-start.47 = (f32[2,1,8,128]{3,2,1,0:T(8,128)S(1)}, f32[2,1,8,128]{3,2,1,0:T(8,128)S(1)}, u32[]{:S(2)}, u32[]{:S(2)}) collective-permute-start(f32[2,1,8,128]{3,2,1,0:T(8,128)S(1)} %get-tuple-element.98), channel_id=1, source_target_pairs={{0,16},{16,32},{32,48},{48,64},{64,80},{80,96},{96,112},{112,128},... | collective-permute-start | bytes 24584 | tf_op jit(solution)/shard_map/ppermute | solution.py:24
  (300 other events, 4980.8 us)
where the time goes:
time: 386 us; the launch traced here: 384 us
  starting transfers between devices  167 us (43%)
  blocking collectives  115 us (30%)
  matrix products  34.2 us (9%)
  local copies, waits for them, and re-layouts  22.1 us (6%)
  waiting for transfers between devices  21.5 us (6%)
  other arithmetic  17.5 us (5%)
  between operations  6.61 us (2%)
    psum x1, blocking collectives, per_device(): summed_flat = lax.psum(flat, ('blk', 'gy', 'rep'))  101 us
    ppermute x24, starting transfers between devices, exchange_faces(): high = lax.ppermute(lax.slice_in_dim(block, 0, 1, axis=dim), axis, backward)  98.7 us
    ppermute x24, starting transfers between devices, exchange_faces(): lax.ppermute(lax.slice_in_dim(block, size - 1, size, axis=dim), axis, for...  68.5 us
    ppermute x24, waiting for transfers between devices, exchange_faces(): lax.ppermute(lax.slice_in_dim(block, size - 1, size, axis=dim), axis, for...  17.3 us
    all_gather x1, blocking collectives, gather_params(): full = lax.all_gather(packed, 'rep', axis=0, tiled=True)  13.3 us
  transfers between devices with their start and end apart: 48, of which 9 were waited for; matrix products, arithmetic and copies ran while one was open for 1% of the time, Pallas kernels for 0%

commit v1 on v0

--- a/solution.py
+++ b/solution.py
@@ -185,7 +185,8 @@
     start_sensitivity = adjoint * (2.0 * total_cells)
     pieces = list(grad_sums) + [loss_part[None]]
     flat = jnp.concatenate([piece.reshape(-1) for piece in pieces])
-    summed_flat = lax.psum(flat, ("blk", "gy", "rep"))
+    partial = lax.psum(flat, "blk")
+    summed_flat = lax.psum(partial, ("gy", "rep"))
     summed = []
     start = 0
     for piece in pieces:

time: 386 us -> 467 us (1.21); the launches traced: 384 us -> 460 us
  blocking collectives: 115 us -> 191 us
    psum x1 -> x2, blocking collectives: 101 us -> 177 us  [the longest x1 90.9 us: per_device(): partial = lax.psum(flat, 'blk')]
where the time goes in v1:
time: 467 us; the launch traced here: 460 us
  blocking collectives  191 us (41%)
  starting transfers between devices  167 us (36%)
  matrix products  34.2 us (7%)
  local copies, waits for them, and re-layouts  22 us (5%)
  waiting for transfers between devices  21.5 us (5%)
  other arithmetic  17.5 us (4%)
  between operations  6.61 us (1%)
    ppermute x24, starting transfers between devices, exchange_faces(): high = lax.ppermute(lax.slice_in_dim(block, 0, 1, axis=dim), axis, backward)  98.6 us
    psum x1, blocking collectives, per_device(): partial = lax.psum(flat, 'blk')  90.9 us
    psum x1, blocking collectives, per_device(): summed_flat = lax.psum(partial, ('gy', 'rep'))  86.4 us
    ppermute x24, starting transfers between devices, exchange_faces(): lax.ppermute(lax.slice_in_dim(block, size - 1, size, axis=dim), axis, for...  68.6 us
    ppermute x24, waiting for transfers between devices, exchange_faces(): lax.ppermute(lax.slice_in_dim(block, size - 1, size, axis=dim), axis, for...  17.3 us
    all_gather x1, blocking collectives, gather_params(): full = lax.all_gather(packed, 'rep', axis=0, tiled=True)  13.3 us
  transfers between devices with their start and end apart: 48, of which 9 were waited for; matrix products, arithmetic and copies ran while one was open for 1% of the time, Pallas kernels for 0%

profile of v1, /device:TPU:1, one launch (start us, length us, event | category | flops | bytes accessed | tf_op | source)
XLA Modules:
  0.0 459.8 jit_solution(5671168981674032787)
XLA Ops:
  5.6 13.3 %all_gather.3 = bf16[64,82]{1,0:T(8,128)(2,1)S(1)} all-gather(bf16[16,82]{1,0:T(8,128)(2,1)S(1)} %concatenate.347), channel_id=1, replica_groups=mesh['blk'=32,'gy'=4,'rep'=4] {'rep'}, dimensions={0}, use_global_device_ids=true | all-gather | bytes 13120 | tf_op jit(solution)/shard_map/all_gather | solution.py:122
  25.0 1.9 collective-permute-start.2
  26.9 3.4 collective-permute-start.3
  30.3 7.8 %collective-permute-start.4 = (f32[4,1,8,128]{3,2,1,0:T(8,128)S(1)}, f32[4,1,8,128]{3,2,1,0:T(8,128)S(1)}, u32[]{:S(2)}, u32[]{:S(2)}) collective-permute-start(f32[4,1,8,128]{3,2,1,0:T(8,128)S(1)} %get-tuple-element.85), channel_id=1, source_target_pairs={{16,0},{32,16},{48,32},{64,48},{80,64},{96,80},{112,96},{128,112},... | collective-permute-start | bytes 49160 | tf_op jit(solution)/shard_map/ppermute | solution.py:25
  38.1 1.9 collective-permute-start.5
  40.1 2.7 collective-permute-start
  43.1 4.2 collective-permute-done
  54.9 5.5 %collective-permute-start.6 = (f32[4,4,8,1]{3,2,1,0:T(8,128)S(1)}, f32[4,4,8,1]{3,2,1,0:T(8,128)S(1)}, u32[]{:S(2)}, u32[]{:S(2)}) collective-permute-start(f32[4,4,8,1]{3,2,1,0:T(8,128)S(1)} %get-tuple-element.69), channel_id=1, source_target_pairs={{1,0},{2,1},{3,2},{0,3},{5,4},{6,5},{7,6},{4,7},{9,8},{10,9},{11,1... | collective-permute-start | bytes 1544 | tf_op jit(solution)/shard_map/ppermute | solution.py:25
  60.4 4.6 collective-permute-start.8
  65.0 1.9 collective-permute-start.9
  66.9 4.9 %collective-permute-start.10 = (f32[4,1,8,128]{3,2,1,0:T(8,128)S(1)}, f32[4,1,8,128]{3,2,1,0:T(8,128)S(1)}, u32[]{:S(2)}, u32[]{:S(2)}) collective-permute-start(f32[4,1,8,128]{3,2,1,0:T(8,128)S(1)} %get-tuple-element.75), channel_id=1, source_target_pairs={{16,0},{32,16},{48,32},{64,48},{80,64},{96,80},{112,96},{128,112},... | collective-permute-start | bytes 49160 | tf_op jit(solution)/shard_map/ppermute | solution.py:25
  73.7 3.9 collective-permute-start.7
  83.5 4.2 collective-permute-start.12
  87.8 4.9 %collective-permute-start.14 = (f32[4,4,1,128]{3,2,1,0:T(1,128)S(1)}, f32[4,4,1,128]{3,2,1,0:T(1,128)S(1)}, u32[]{:S(2)}, u32[]{:S(2)}) collective-permute-start(f32[4,4,1,128]{3,2,1,0:T(1,128)S(1)} %get-tuple-element.63), channel_id=1, source_target_pairs={{4,0},{8,4},{12,8},{0,12},{5,1},{9,5},{13,9},{1,13},{6,2},{10,6},{... | collective-permute-start | bytes 24584 | tf_op jit(solution)/shard_map/ppermute | solution.py:25
  94.6 5.8 %collective-permute-start.16 = (f32[4,1,8,128]{3,2,1,0:T(8,128)S(1)}, f32[4,1,8,128]{3,2,1,0:T(8,128)S(1)}, u32[]{:S(2)}, u32[]{:S(2)}) collective-permute-start(f32[4,1,8,128]{3,2,1,0:T(8,128)S(1)} %get-tuple-element.65), channel_id=1, source_target_pairs={{16,0},{32,16},{48,32},{64,48},{80,64},{96,80},{112,96},{128,112},... | collective-permute-start | bytes 49160 | tf_op jit(solution)/shard_map/ppermute | solution.py:25
  100.3 1.9 collective-permute-start.17
  102.3 4.0 collective-permute-start.13
  111.7 4.2 collective-permute-start.18
  116.0 4.9 %collective-permute-start.20 = (f32[4,4,1,128]{3,2,1,0:T(1,128)S(1)}, f32[4,4,1,128]{3,2,1,0:T(1,128)S(1)}, u32[]{:S(2)}, u32[]{:S(2)}) collective-permute-start(f32[4,4,1,128]{3,2,1,0:T(1,128)S(1)} %get-tuple-element.53), channel_id=1, source_target_pairs={{4,0},{8,4},{12,8},{0,12},{5,1},{9,5},{13,9},{1,13},{6,2},{10,6},{... | collective-permute-start | bytes 24584 | tf_op jit(solution)/shard_map/ppermute | solution.py:25
  122.8 5.7 %collective-permute-start.22 = (f32[4,1,8,128]{3,2,1,0:T(8,128)S(1)}, f32[4,1,8,128]{3,2,1,0:T(8,128)S(1)}, u32[]{:S(2)}, u32[]{:S(2)}) collective-permute-start(f32[4,1,8,128]{3,2,1,0:T(8,128)S(1)} %get-tuple-element.55), channel_id=1, source_target_pairs={{16,0},{32,16},{48,32},{64,48},{80,64},{96,80},{112,96},{128,112},... | collective-permute-start | bytes 49160 | tf_op jit(solution)/shard_map/ppermute | solution.py:25
  130.5 4.0 collective-permute-start.19
  140.1 4.8 %collective-permute-start.26 = (f32[2,4,1,128]{3,2,1,0:T(1,128)}, f32[2,4,1,128]{3,2,1,0:T(1,128)}, u32[]{:S(2)}, u32[]{:S(2)}) collective-permute-start(f32[2,4,1,128]{3,2,1,0:T(1,128)} %get-tuple-element.129), channel_id=1, source_target_pairs={{4,0},{8,4},{12,8},{0,12},{5,1},{9,5},{13,9},{1,13},{6,2},{10,6},{... | collective-permute-start | bytes 12296 | tf_op jit(solution)/shard_map/ppermute | solution.py:25
  144.9 1.9 collective-permute-start.27
  147.5 5.1 %collective-permute-start.28 = (f32[2,1,8,128]{3,2,1,0:T(8,128)}, f32[2,1,8,128]{3,2,1,0:T(8,128)}, u32[]{:S(2)}, u32[]{:S(2)}) collective-permute-start(f32[2,1,8,128]{3,2,1,0:T(8,128)} %get-tuple-element.133), channel_id=1, source_target_pairs={{16,0},{32,16},{48,32},{64,48},{80,64},{96,80},{112,96},{128,112},... | collective-permute-start | bytes 24584 | tf_op jit(solution)/shard_map/ppermute | solution.py:25
  152.6 5.4 %collective-permute-start.24 = (f32[2,4,8,1]{3,2,1,0:T(8,128)}, f32[2,4,8,1]{3,2,1,0:T(8,128)}, u32[]{:S(2)}, u32[]{:S(2)}) collective-permute-start(f32[2,4,8,1]{3,2,1,0:T(8,128)} %get-tuple-element.125), channel_id=1, source_target_pairs={{1,0},{2,1},{3,2},{0,3},{5,4},{6,5},{7,6},{4,7},{9,8},{10,9},{11,1... | collective-permute-start | bytes 776 | tf_op jit(solution)/shard_map/ppermute | solution.py:25
  158.1 3.4 collective-permute-start.25
  165.2 3.7 collective-permute-done.29
  173.7 2.1 fusion.34
  181.7 4.8 %collective-permute-start.32 = (f32[2,4,1,128]{3,2,1,0:T(1,128)S(1)}, f32[2,4,1,128]{3,2,1,0:T(1,128)S(1)}, u32[]{:S(2)}, u32[]{:S(2)}) collective-permute-start(f32[2,4,1,128]{3,2,1,0:T(1,128)S(1)} %get-tuple-element.117), channel_id=1, source_target_pairs={{4,0},{8,4},{12,8},{0,12},{5,1},{9,5},{13,9},{1,13},{6,2},{10,6},{... | collective-permute-start | bytes 12296 | tf_op jit(solution)/shard_map/ppermute | solution.py:25
  188.5 2.4 collective-permute-start.30
  190.9 4.7 %collective-permute-start.31 = (f32[2,4,8,1]{3,2,1,0:T(8,128)S(1)}, f32[2,4,8,1]{3,2,1,0:T(8,128)S(1)}, u32[]{:S(2)}, u32[]{:S(2)}) collective-permute-start(f32[2,4,8,1]{3,2,1,0:T(8,128)S(1)} %get-tuple-element.114), channel_id=1, source_target_pairs={{0,1},{1,2},{2,3},{3,0},{4,5},{5,6},{6,7},{7,4},{8,9},{9,10},{10,1... | collective-permute-start | bytes 776 | tf_op jit(solution)/shard_map/ppermute | solution.py:24
  197.5 3.5 collective-permute-start.35
  201.4 2.7 collective-permute-done.35
  208.5 2.2 convert_reduce_fusion.2
  215.9 4.6 collective-permute-start.38
  220.5 1.9 collective-permute-start.39
  224.4 5.1 %collective-permute-start.37 = (f32[2,4,8,1]{3,2,1,0:T(8,128)S(1)}, f32[2,4,8,1]{3,2,1,0:T(8,128)S(1)}, u32[]{:S(2)}, u32[]{:S(2)}) collective-permute-start(f32[2,4,8,1]{3,2,1,0:T(8,128)S(1)} %get-tuple-element.102), channel_id=1, source_target_pairs={{0,1},{1,2},{2,3},{3,0},{4,5},{5,6},{6,7},{7,4},{8,9},{9,10},{10,1... | collective-permute-start | bytes 776 | tf_op jit(solution)/shard_map/ppermute | solution.py:24
  231.5 3.4 collective-permute-start.41
  235.2 2.8 collective-permute-done.41
  242.3 2.2 convert_reduce_fusion.1
  249.8 4.6 collective-permute-start.44
  256.3 2.2 collective-permute-start.42
  258.6 4.8 %collective-permute-start.43 = (f32[2,4,8,1]{3,2,1,0:T(8,128)S(1)}, f32[2,4,8,1]{3,2,1,0:T(8,128)S(1)}, u32[]{:S(2)}, u32[]{:S(2)}) collective-permute-start(f32[2,4,8,1]{3,2,1,0:T(8,128)S(1)} %get-tuple-element.90), channel_id=1, source_target_pairs={{0,1},{1,2},{2,3},{3,0},{4,5},{5,6},{6,7},{7,4},{8,9},{9,10},{10,1... | collective-permute-start | bytes 776 | tf_op jit(solution)/shard_map/ppermute | solution.py:24
  263.4 1.9 collective-permute-start.46
  265.3 3.4 collective-permute-start.47
  269.0 2.8 collective-permute-done.47
  276.9 90.9 %psum.14 = f32[5255]{0:T(1024)S(1)} all-reduce(f32[5255]{0:T(1024)S(1)} %concatenate.436), channel_id=1, replica_groups=mesh['blk'=32,'gy'=4,'rep'=4] {'blk'}, use_global_device_ids=true, to_apply=%region_13.0 | all-reduce | flops 5255 | bytes 42040 | tf_op jit(solution)/shard_map/psum | solution.py:188
  367.9 86.4 %psum.15 = f32[5255]{0:T(1024)S(1)} all-reduce(f32[5255]{0:T(1024)S(1)} %psum.14), channel_id=1, replica_groups=mesh['blk'=32,'gy'=4,'rep'=4] {'gy','rep'}, use_global_device_ids=true, to_apply=%region_14.0 | all-reduce | flops 5255 | bytes 42040 | tf_op jit(solution)/shard_map/psum | solution.py:189
  (852 shorter events, 93.8 us)
Async XLA Ops:
  25.0 25.5 %collective-permute-start.2 = (f32[4,4,1,128]{3,2,1,0:T(1,128)S(1)}, f32[4,4,1,128]{3,2,1,0:T(1,128)S(1)}, u32[]{:S(2)}, u32[]{:S(2)}) collective-permute-start(f32[4,4,1,128]{3,2,1,0:T(1,128)S(1)} %get-tuple-element.83), channel_id=1, source_target_pairs={{4,0},{8,4},{12,8},{0,12},{5,1},{9,5},{13,9},{1,13},{6,2},{10,6},{... | collective-permute-start | bytes 24584 | tf_op jit(solution)/shard_map/ppermute | solution.py:25
  26.9 23.6 %collective-permute-start.3 = (f32[4,4,1,128]{3,2,1,0:T(1,128)S(1)}, f32[4,4,1,128]{3,2,1,0:T(1,128)S(1)}, u32[]{:S(2)}, u32[]{:S(2)}) collective-permute-start(f32[4,4,1,128]{3,2,1,0:T(1,128)S(1)} %get-tuple-element.84), channel_id=1, source_target_pairs={{0,4},{4,8},{8,12},{12,0},{1,5},{5,9},{9,13},{13,1},{2,6},{6,10},{... | collective-permute-start | bytes 24584 | tf_op jit(solution)/shard_map/ppermute | solution.py:24
  30.3 20.2 %collective-permute-start.4 = (f32[4,1,8,128]{3,2,1,0:T(8,128)S(1)}, f32[4,1,8,128]{3,2,1,0:T(8,128)S(1)}, u32[]{:S(2)}, u32[]{:S(2)}) collective-permute-start(f32[4,1,8,128]{3,2,1,0:T(8,128)S(1)} %get-tuple-element.85), channel_id=1, source_target_pairs={{16,0},{32,16},{48,32},{64,48},{80,64},{96,80},{112,96},{128,112},... | collective-permute-start | bytes 49160 | tf_op jit(solution)/shard_map/ppermute | solution.py:25
  38.1 12.5 %collective-permute-start.5 = (f32[4,1,8,128]{3,2,1,0:T(8,128)S(1)}, f32[4,1,8,128]{3,2,1,0:T(8,128)S(1)}, u32[]{:S(2)}, u32[]{:S(2)}) collective-permute-start(f32[4,1,8,128]{3,2,1,0:T(8,128)S(1)} %get-tuple-element.86), channel_id=1, source_target_pairs={{0,16},{16,32},{32,48},{48,64},{64,80},{80,96},{96,112},{112,128},... | collective-permute-start | bytes 49160 | tf_op jit(solution)/shard_map/ppermute | solution.py:24
  40.1 7.1 %collective-permute-start = (f32[4,4,8,1]{3,2,1,0:T(8,128)S(1)}, f32[4,4,8,1]{3,2,1,0:T(8,128)S(1)}, u32[]{:S(2)}, u32[]{:S(2)}) collective-permute-start(f32[4,4,8,1]{3,2,1,0:T(8,128)S(1)} %get-tuple-element.79), channel_id=1, source_target_pairs={{1,0},{2,1},{3,2},{0,3},{5,4},{6,5},{7,6},{4,7},{9,8},{10,9},{11,1... | collective-permute-start | bytes 1544 | tf_op jit(solution)/shard_map/ppermute | solution.py:25
  47.2 3.2 collective-permute-start.1
  54.9 18.9 %collective-permute-start.6 = (f32[4,4,8,1]{3,2,1,0:T(8,128)S(1)}, f32[4,4,8,1]{3,2,1,0:T(8,128)S(1)}, u32[]{:S(2)}, u32[]{:S(2)}) collective-permute-start(f32[4,4,8,1]{3,2,1,0:T(8,128)S(1)} %get-tuple-element.69), channel_id=1, source_target_pairs={{1,0},{2,1},{3,2},{0,3},{5,4},{6,5},{7,6},{4,7},{9,8},{10,9},{11,1... | collective-permute-start | bytes 1544 | tf_op jit(solution)/shard_map/ppermute | solution.py:25
  60.4 18.6 %collective-permute-start.8 = (f32[4,4,1,128]{3,2,1,0:T(1,128)S(1)}, f32[4,4,1,128]{3,2,1,0:T(1,128)S(1)}, u32[]{:S(2)}, u32[]{:S(2)}) collective-permute-start(f32[4,4,1,128]{3,2,1,0:T(1,128)S(1)} %get-tuple-element.73), channel_id=1, source_target_pairs={{4,0},{8,4},{12,8},{0,12},{5,1},{9,5},{13,9},{1,13},{6,2},{10,6},{... | collective-permute-start | bytes 24584 | tf_op jit(solution)/shard_map/ppermute | solution.py:25
  65.0 14.1 %collective-permute-start.9 = (f32[4,4,1,128]{3,2,1,0:T(1,128)S(1)}, f32[4,4,1,128]{3,2,1,0:T(1,128)S(1)}, u32[]{:S(2)}, u32[]{:S(2)}) collective-permute-start(f32[4,4,1,128]{3,2,1,0:T(1,128)S(1)} %get-tuple-element.74), channel_id=1, source_target_pairs={{0,4},{4,8},{8,12},{12,0},{1,5},{5,9},{9,13},{13,1},{2,6},{6,10},{... | collective-permute-start | bytes 24584 | tf_op jit(solution)/shard_map/ppermute | solution.py:24
  66.9 12.2 %collective-permute-start.10 = (f32[4,1,8,128]{3,2,1,0:T(8,128)S(1)}, f32[4,1,8,128]{3,2,1,0:T(8,128)S(1)}, u32[]{:S(2)}, u32[]{:S(2)}) collective-permute-start(f32[4,1,8,128]{3,2,1,0:T(8,128)S(1)} %get-tuple-element.75), channel_id=1, source_target_pairs={{16,0},{32,16},{48,32},{64,48},{80,64},{96,80},{112,96},{128,112},... | collective-permute-start | bytes 49160 | tf_op jit(solution)/shard_map/ppermute | solution.py:25
  71.8 7.4 %collective-permute-start.11 = (f32[4,1,8,128]{3,2,1,0:T(8,128)S(1)}, f32[4,1,8,128]{3,2,1,0:T(8,128)S(1)}, u32[]{:S(2)}, u32[]{:S(2)}) collective-permute-start(f32[4,1,8,128]{3,2,1,0:T(8,128)S(1)} %get-tuple-element.76), channel_id=1, source_target_pairs={{0,16},{16,32},{32,48},{48,64},{64,80},{80,96},{96,112},{112,128},... | collective-permute-start | bytes 49160 | tf_op jit(solution)/shard_map/ppermute | solution.py:24
  73.7 5.3 %collective-permute-start.7 = (f32[4,4,8,1]{3,2,1,0:T(8,128)S(1)}, f32[4,4,8,1]{3,2,1,0:T(8,128)S(1)}, u32[]{:S(2)}, u32[]{:S(2)}) collective-permute-start(f32[4,4,8,1]{3,2,1,0:T(8,128)S(1)} %get-tuple-element.70), channel_id=1, source_target_pairs={{0,1},{1,2},{2,3},{3,0},{4,5},{5,6},{6,7},{7,4},{8,9},{9,10},{10,1... | collective-permute-start | bytes 1544 | tf_op jit(solution)/shard_map/ppermute | solution.py:24
  83.5 18.7 %collective-permute-start.12 = (f32[4,4,8,1]{3,2,1,0:T(8,128)S(1)}, f32[4,4,8,1]{3,2,1,0:T(8,128)S(1)}, u32[]{:S(2)}, u32[]{:S(2)}) collective-permute-start(f32[4,4,8,1]{3,2,1,0:T(8,128)S(1)} %get-tuple-element.59), channel_id=1, source_target_pairs={{1,0},{2,1},{3,2},{0,3},{5,4},{6,5},{7,6},{4,7},{9,8},{10,9},{11,1... | collective-permute-start | bytes 1544 | tf_op jit(solution)/shard_map/ppermute | solution.py:25
  87.8 19.8 %collective-permute-start.14 = (f32[4,4,1,128]{3,2,1,0:T(1,128)S(1)}, f32[4,4,1,128]{3,2,1,0:T(1,128)S(1)}, u32[]{:S(2)}, u32[]{:S(2)}) collective-permute-start(f32[4,4,1,128]{3,2,1,0:T(1,128)S(1)} %get-tuple-element.63), channel_id=1, source_target_pairs={{4,0},{8,4},{12,8},{0,12},{5,1},{9,5},{13,9},{1,13},{6,2},{10,6},{... | collective-permute-start | bytes 24584 | tf_op jit(solution)/shard_map/ppermute | solution.py:25
  92.6 15.0 %collective-permute-start.15 = (f32[4,4,1,128]{3,2,1,0:T(1,128)S(1)}, f32[4,4,1,128]{3,2,1,0:T(1,128)S(1)}, u32[]{:S(2)}, u32[]{:S(2)}) collective-permute-start(f32[4,4,1,128]{3,2,1,0:T(1,128)S(1)} %get-tuple-element.64), channel_id=1, source_target_pairs={{0,4},{4,8},{8,12},{12,0},{1,5},{5,9},{9,13},{13,1},{2,6},{6,10},{... | collective-permute-start | bytes 24584 | tf_op jit(solution)/shard_map/ppermute | solution.py:24
  94.6 13.1 %collective-permute-start.16 = (f32[4,1,8,128]{3,2,1,0:T(8,128)S(1)}, f32[4,1,8,128]{3,2,1,0:T(8,128)S(1)}, u32[]{:S(2)}, u32[]{:S(2)}) collective-permute-start(f32[4,1,8,128]{3,2,1,0:T(8,128)S(1)} %get-tuple-element.65), channel_id=1, source_target_pairs={{16,0},{32,16},{48,32},{64,48},{80,64},{96,80},{112,96},{128,112},... | collective-permute-start | bytes 49160 | tf_op jit(solution)/shard_map/ppermute | solution.py:25
  100.3 7.4 %collective-permute-start.17 = (f32[4,1,8,128]{3,2,1,0:T(8,128)S(1)}, f32[4,1,8,128]{3,2,1,0:T(8,128)S(1)}, u32[]{:S(2)}, u32[]{:S(2)}) collective-permute-start(f32[4,1,8,128]{3,2,1,0:T(8,128)S(1)} %get-tuple-element.66), channel_id=1, source_target_pairs={{0,16},{16,32},{32,48},{48,64},{64,80},{80,96},{96,112},{112,128},... | collective-permute-start | bytes 49160 | tf_op jit(solution)/shard_map/ppermute | solution.py:24
  102.3 5.3 %collective-permute-start.13 = (f32[4,4,8,1]{3,2,1,0:T(8,128)S(1)}, f32[4,4,8,1]{3,2,1,0:T(8,128)S(1)}, u32[]{:S(2)}, u32[]{:S(2)}) collective-permute-start(f32[4,4,8,1]{3,2,1,0:T(8,128)S(1)} %get-tuple-element.60), channel_id=1, source_target_pairs={{0,1},{1,2},{2,3},{3,0},{4,5},{5,6},{6,7},{7,4},{8,9},{9,10},{10,1... | collective-permute-start | bytes 1544 | tf_op jit(solution)/shard_map/ppermute | solution.py:24
  111.7 18.7 %collective-permute-start.18 = (f32[4,4,8,1]{3,2,1,0:T(8,128)S(1)}, f32[4,4,8,1]{3,2,1,0:T(8,128)S(1)}, u32[]{:S(2)}, u32[]{:S(2)}) collective-permute-start(f32[4,4,8,1]{3,2,1,0:T(8,128)S(1)} %get-tuple-element.49), channel_id=1, source_target_pairs={{1,0},{2,1},{3,2},{0,3},{5,4},{6,5},{7,6},{4,7},{9,8},{10,9},{11,1... | collective-permute-start | bytes 1544 | tf_op jit(solution)/shard_map/ppermute | solution.py:25
  116.0 19.9 %collective-permute-start.20 = (f32[4,4,1,128]{3,2,1,0:T(1,128)S(1)}, f32[4,4,1,128]{3,2,1,0:T(1,128)S(1)}, u32[]{:S(2)}, u32[]{:S(2)}) collective-permute-start(f32[4,4,1,128]{3,2,1,0:T(1,128)S(1)} %get-tuple-element.53), channel_id=1, source_target_pairs={{4,0},{8,4},{12,8},{0,12},{5,1},{9,5},{13,9},{1,13},{6,2},{10,6},{... | collective-permute-start | bytes 24584 | tf_op jit(solution)/shard_map/ppermute | solution.py:25
  120.8 15.0 %collective-permute-start.21 = (f32[4,4,1,128]{3,2,1,0:T(1,128)S(1)}, f32[4,4,1,128]{3,2,1,0:T(1,128)S(1)}, u32[]{:S(2)}, u32[]{:S(2)}) collective-permute-start(f32[4,4,1,128]{3,2,1,0:T(1,128)S(1)} %get-tuple-element.54), channel_id=1, source_target_pairs={{0,4},{4,8},{8,12},{12,0},{1,5},{5,9},{9,13},{13,1},{2,6},{6,10},{... | collective-permute-start | bytes 24584 | tf_op jit(solution)/shard_map/ppermute | solution.py:24
  122.8 13.1 %collective-permute-start.22 = (f32[4,1,8,128]{3,2,1,0:T(8,128)S(1)}, f32[4,1,8,128]{3,2,1,0:T(8,128)S(1)}, u32[]{:S(2)}, u32[]{:S(2)}) collective-permute-start(f32[4,1,8,128]{3,2,1,0:T(8,128)S(1)} %get-tuple-element.55), channel_id=1, source_target_pairs={{16,0},{32,16},{48,32},{64,48},{80,64},{96,80},{112,96},{128,112},... | collective-permute-start | bytes 49160 | tf_op jit(solution)/shard_map/ppermute | solution.py:25
  128.5 7.4 %collective-permute-start.23 = (f32[4,1,8,128]{3,2,1,0:T(8,128)S(1)}, f32[4,1,8,128]{3,2,1,0:T(8,128)S(1)}, u32[]{:S(2)}, u32[]{:S(2)}) collective-permute-start(f32[4,1,8,128]{3,2,1,0:T(8,128)S(1)} %get-tuple-element.56), channel_id=1, source_target_pairs={{0,16},{16,32},{32,48},{48,64},{64,80},{80,96},{96,112},{112,128},... | collective-permute-start | bytes 49160 | tf_op jit(solution)/shard_map/ppermute | solution.py:24
  130.5 5.4 %collective-permute-start.19 = (f32[4,4,8,1]{3,2,1,0:T(8,128)S(1)}, f32[4,4,8,1]{3,2,1,0:T(8,128)S(1)}, u32[]{:S(2)}, u32[]{:S(2)}) collective-permute-start(f32[4,4,8,1]{3,2,1,0:T(8,128)S(1)} %get-tuple-element.50), channel_id=1, source_target_pairs={{0,1},{1,2},{2,3},{3,0},{4,5},{5,6},{6,7},{7,4},{8,9},{9,10},{10,1... | collective-permute-start | bytes 1544 | tf_op jit(solution)/shard_map/ppermute | solution.py:24
  140.1 24.1 %collective-permute-start.26 = (f32[2,4,1,128]{3,2,1,0:T(1,128)}, f32[2,4,1,128]{3,2,1,0:T(1,128)}, u32[]{:S(2)}, u32[]{:S(2)}) collective-permute-start(f32[2,4,1,128]{3,2,1,0:T(1,128)} %get-tuple-element.129), channel_id=1, source_target_pairs={{4,0},{8,4},{12,8},{0,12},{5,1},{9,5},{13,9},{1,13},{6,2},{10,6},{... | collective-permute-start | bytes 12296 | tf_op jit(solution)/shard_map/ppermute | solution.py:25
  144.9 19.2 %collective-permute-start.27 = (f32[2,4,1,128]{3,2,1,0:T(1,128)}, f32[2,4,1,128]{3,2,1,0:T(1,128)}, u32[]{:S(2)}, u32[]{:S(2)}) collective-permute-start(f32[2,4,1,128]{3,2,1,0:T(1,128)} %get-tuple-element.130), channel_id=1, source_target_pairs={{0,4},{4,8},{8,12},{12,0},{1,5},{5,9},{9,13},{13,1},{2,6},{6,10},{... | collective-permute-start | bytes 12296 | tf_op jit(solution)/shard_map/ppermute | solution.py:24
  147.5 17.7 %collective-permute-start.28 = (f32[2,1,8,128]{3,2,1,0:T(8,128)}, f32[2,1,8,128]{3,2,1,0:T(8,128)}, u32[]{:S(2)}, u32[]{:S(2)}) collective-permute-start(f32[2,1,8,128]{3,2,1,0:T(8,128)} %get-tuple-element.133), channel_id=1, source_target_pairs={{16,0},{32,16},{48,32},{64,48},{80,64},{96,80},{112,96},{128,112},... | collective-permute-start | bytes 24584 | tf_op jit(solution)/shard_map/ppermute | solution.py:25
  152.6 9.6 %collective-permute-start.24 = (f32[2,4,8,1]{3,2,1,0:T(8,128)}, f32[2,4,8,1]{3,2,1,0:T(8,128)}, u32[]{:S(2)}, u32[]{:S(2)}) collective-permute-start(f32[2,4,8,1]{3,2,1,0:T(8,128)} %get-tuple-element.125), channel_id=1, source_target_pairs={{1,0},{2,1},{3,2},{0,3},{5,4},{6,5},{7,6},{4,7},{9,8},{10,9},{11,1... | collective-permute-start | bytes 776 | tf_op jit(solution)/shard_map/ppermute | solution.py:25
  158.1 6.1 %collective-permute-start.25 = (f32[2,4,8,1]{3,2,1,0:T(8,128)}, f32[2,4,8,1]{3,2,1,0:T(8,128)}, u32[]{:S(2)}, u32[]{:S(2)}) collective-permute-start(f32[2,4,8,1]{3,2,1,0:T(8,128)} %get-tuple-element.126), channel_id=1, source_target_pairs={{0,1},{1,2},{2,3},{3,0},{4,5},{5,6},{6,7},{7,4},{8,9},{9,10},{10,1... | collective-permute-start | bytes 776 | tf_op jit(solution)/shard_map/ppermute | solution.py:24
  162.2 6.7 %collective-permute-start.29 = (f32[2,1,8,128]{3,2,1,0:T(8,128)}, f32[2,1,8,128]{3,2,1,0:T(8,128)S(1)}, u32[]{:S(2)}, u32[]{:S(2)}) collective-permute-start(f32[2,1,8,128]{3,2,1,0:T(8,128)} %get-tuple-element.134), channel_id=1, source_target_pairs={{0,16},{16,32},{32,48},{48,64},{64,80},{80,96},{96,112},{112,128},... | collective-permute-start | bytes 24584 | tf_op jit(solution)/shard_map/ppermute | solution.py:24
  181.7 19.4 %collective-permute-start.32 = (f32[2,4,1,128]{3,2,1,0:T(1,128)S(1)}, f32[2,4,1,128]{3,2,1,0:T(1,128)S(1)}, u32[]{:S(2)}, u32[]{:S(2)}) collective-permute-start(f32[2,4,1,128]{3,2,1,0:T(1,128)S(1)} %get-tuple-element.117), channel_id=1, source_target_pairs={{4,0},{8,4},{12,8},{0,12},{5,1},{9,5},{13,9},{1,13},{6,2},{10,6},{... | collective-permute-start | bytes 12296 | tf_op jit(solution)/shard_map/ppermute | solution.py:25
  186.6 14.6 %collective-permute-start.33 = (f32[2,4,1,128]{3,2,1,0:T(1,128)S(1)}, f32[2,4,1,128]{3,2,1,0:T(1,128)S(1)}, u32[]{:S(2)}, u32[]{:S(2)}) collective-permute-start(f32[2,4,1,128]{3,2,1,0:T(1,128)S(1)} %get-tuple-element.118), channel_id=1, source_target_pairs={{0,4},{4,8},{8,12},{12,0},{1,5},{5,9},{9,13},{13,1},{2,6},{6,10},{... | collective-permute-start | bytes 12296 | tf_op jit(solution)/shard_map/ppermute | solution.py:24
  188.5 9.0 %collective-permute-start.30 = (f32[2,4,8,1]{3,2,1,0:T(8,128)S(1)}, f32[2,4,8,1]{3,2,1,0:T(8,128)S(1)}, u32[]{:S(2)}, u32[]{:S(2)}) collective-permute-start(f32[2,4,8,1]{3,2,1,0:T(8,128)S(1)} %get-tuple-element.113), channel_id=1, source_target_pairs={{1,0},{2,1},{3,2},{0,3},{5,4},{6,5},{7,6},{4,7},{9,8},{10,9},{11,1... | collective-permute-start | bytes 776 | tf_op jit(solution)/shard_map/ppermute | solution.py:25
  190.9 10.2 %collective-permute-start.31 = (f32[2,4,8,1]{3,2,1,0:T(8,128)S(1)}, f32[2,4,8,1]{3,2,1,0:T(8,128)S(1)}, u32[]{:S(2)}, u32[]{:S(2)}) collective-permute-start(f32[2,4,8,1]{3,2,1,0:T(8,128)S(1)} %get-tuple-element.114), channel_id=1, source_target_pairs={{0,1},{1,2},{2,3},{3,0},{4,5},{5,6},{6,7},{7,4},{8,9},{9,10},{10,1... | collective-permute-start | bytes 776 | tf_op jit(solution)/shard_map/ppermute | solution.py:24
  195.6 5.8 %collective-permute-start.34 = (f32[2,1,8,128]{3,2,1,0:T(8,128)S(1)}, f32[2,1,8,128]{3,2,1,0:T(8,128)S(1)}, u32[]{:S(2)}, u32[]{:S(2)}) collective-permute-start(f32[2,1,8,128]{3,2,1,0:T(8,128)S(1)} %get-tuple-element.121), channel_id=1, source_target_pairs={{16,0},{32,16},{48,32},{64,48},{80,64},{96,80},{112,96},{128,112},... | collective-permute-start | bytes 24584 | tf_op jit(solution)/shard_map/ppermute | solution.py:25
  197.5 6.5 %collective-permute-start.35 = (f32[2,1,8,128]{3,2,1,0:T(8,128)S(1)}, f32[2,1,8,128]{3,2,1,0:T(8,128)S(1)}, u32[]{:S(2)}, u32[]{:S(2)}) collective-permute-start(f32[2,1,8,128]{3,2,1,0:T(8,128)S(1)} %get-tuple-element.122), channel_id=1, source_target_pairs={{0,16},{16,32},{32,48},{48,64},{64,80},{80,96},{96,112},{112,128},... | collective-permute-start | bytes 24584 | tf_op jit(solution)/shard_map/ppermute | solution.py:24
  215.9 18.9 %collective-permute-start.38 = (f32[2,4,1,128]{3,2,1,0:T(1,128)S(1)}, f32[2,4,1,128]{3,2,1,0:T(1,128)S(1)}, u32[]{:S(2)}, u32[]{:S(2)}) collective-permute-start(f32[2,4,1,128]{3,2,1,0:T(1,128)S(1)} %get-tuple-element.105), channel_id=1, source_target_pairs={{4,0},{8,4},{12,8},{0,12},{5,1},{9,5},{13,9},{1,13},{6,2},{10,6},{... | collective-permute-start | bytes 12296 | tf_op jit(solution)/shard_map/ppermute | solution.py:25
  220.5 14.4 %collective-permute-start.39 = (f32[2,4,1,128]{3,2,1,0:T(1,128)S(1)}, f32[2,4,1,128]{3,2,1,0:T(1,128)S(1)}, u32[]{:S(2)}, u32[]{:S(2)}) collective-permute-start(f32[2,4,1,128]{3,2,1,0:T(1,128)S(1)} %get-tuple-element.106), channel_id=1, source_target_pairs={{0,4},{4,8},{8,12},{12,0},{1,5},{5,9},{9,13},{13,1},{2,6},{6,10},{... | collective-permute-start | bytes 12296 | tf_op jit(solution)/shard_map/ppermute | solution.py:24
  222.5 9.0 %collective-permute-start.36 = (f32[2,4,8,1]{3,2,1,0:T(8,128)S(1)}, f32[2,4,8,1]{3,2,1,0:T(8,128)S(1)}, u32[]{:S(2)}, u32[]{:S(2)}) collective-permute-start(f32[2,4,8,1]{3,2,1,0:T(8,128)S(1)} %get-tuple-element.101), channel_id=1, source_target_pairs={{1,0},{2,1},{3,2},{0,3},{5,4},{6,5},{7,6},{4,7},{9,8},{10,9},{11,1... | collective-permute-start | bytes 776 | tf_op jit(solution)/shard_map/ppermute | solution.py:25
  224.4 10.5 %collective-permute-start.37 = (f32[2,4,8,1]{3,2,1,0:T(8,128)S(1)}, f32[2,4,8,1]{3,2,1,0:T(8,128)S(1)}, u32[]{:S(2)}, u32[]{:S(2)}) collective-permute-start(f32[2,4,8,1]{3,2,1,0:T(8,128)S(1)} %get-tuple-element.102), channel_id=1, source_target_pairs={{0,1},{1,2},{2,3},{3,0},{4,5},{5,6},{6,7},{7,4},{8,9},{9,10},{10,1... | collective-permute-start | bytes 776 | tf_op jit(solution)/shard_map/ppermute | solution.py:24
  229.5 5.6 %collective-permute-start.40 = (f32[2,1,8,128]{3,2,1,0:T(8,128)S(1)}, f32[2,1,8,128]{3,2,1,0:T(8,128)S(1)}, u32[]{:S(2)}, u32[]{:S(2)}) collective-permute-start(f32[2,1,8,128]{3,2,1,0:T(8,128)S(1)} %get-tuple-element.109), channel_id=1, source_target_pairs={{16,0},{32,16},{48,32},{64,48},{80,64},{96,80},{112,96},{128,112},... | collective-permute-start | bytes 24584 | tf_op jit(solution)/shard_map/ppermute | solution.py:25
  231.5 6.5 %collective-permute-start.41 = (f32[2,1,8,128]{3,2,1,0:T(8,128)S(1)}, f32[2,1,8,128]{3,2,1,0:T(8,128)S(1)}, u32[]{:S(2)}, u32[]{:S(2)}) collective-permute-start(f32[2,1,8,128]{3,2,1,0:T(8,128)S(1)} %get-tuple-element.110), channel_id=1, source_target_pairs={{0,16},{16,32},{32,48},{48,64},{64,80},{80,96},{96,112},{112,128},... | collective-permute-start | bytes 24584 | tf_op jit(solution)/shard_map/ppermute | solution.py:24
  249.8 18.9 %collective-permute-start.44 = (f32[2,4,1,128]{3,2,1,0:T(1,128)S(1)}, f32[2,4,1,128]{3,2,1,0:T(1,128)S(1)}, u32[]{:S(2)}, u32[]{:S(2)}) collective-permute-start(f32[2,4,1,128]{3,2,1,0:T(1,128)S(1)} %get-tuple-element.93), channel_id=1, source_target_pairs={{4,0},{8,4},{12,8},{0,12},{5,1},{9,5},{13,9},{1,13},{6,2},{10,6},{... | collective-permute-start | bytes 12296 | tf_op jit(solution)/shard_map/ppermute | solution.py:25
  254.4 14.4 %collective-permute-start.45 = (f32[2,4,1,128]{3,2,1,0:T(1,128)S(1)}, f32[2,4,1,128]{3,2,1,0:T(1,128)S(1)}, u32[]{:S(2)}, u32[]{:S(2)}) collective-permute-start(f32[2,4,1,128]{3,2,1,0:T(1,128)S(1)} %get-tuple-element.94), channel_id=1, source_target_pairs={{0,4},{4,8},{8,12},{12,0},{1,5},{5,9},{9,13},{13,1},{2,6},{6,10},{... | collective-permute-start | bytes 12296 | tf_op jit(solution)/shard_map/ppermute | solution.py:24
  256.3 9.0 %collective-permute-start.42 = (f32[2,4,8,1]{3,2,1,0:T(8,128)S(1)}, f32[2,4,8,1]{3,2,1,0:T(8,128)S(1)}, u32[]{:S(2)}, u32[]{:S(2)}) collective-permute-start(f32[2,4,8,1]{3,2,1,0:T(8,128)S(1)} %get-tuple-element.89), channel_id=1, source_target_pairs={{1,0},{2,1},{3,2},{0,3},{5,4},{6,5},{7,6},{4,7},{9,8},{10,9},{11,1... | collective-permute-start | bytes 776 | tf_op jit(solution)/shard_map/ppermute | solution.py:25
  258.6 10.2 %collective-permute-start.43 = (f32[2,4,8,1]{3,2,1,0:T(8,128)S(1)}, f32[2,4,8,1]{3,2,1,0:T(8,128)S(1)}, u32[]{:S(2)}, u32[]{:S(2)}) collective-permute-start(f32[2,4,8,1]{3,2,1,0:T(8,128)S(1)} %get-tuple-element.90), channel_id=1, source_target_pairs={{0,1},{1,2},{2,3},{3,0},{4,5},{5,6},{6,7},{7,4},{8,9},{9,10},{10,1... | collective-permute-start | bytes 776 | tf_op jit(solution)/shard_map/ppermute | solution.py:24
  263.4 5.6 %collective-permute-start.46 = (f32[2,1,8,128]{3,2,1,0:T(8,128)S(1)}, f32[2,1,8,128]{3,2,1,0:T(8,128)S(1)}, u32[]{:S(2)}, u32[]{:S(2)}) collective-permute-start(f32[2,1,8,128]{3,2,1,0:T(8,128)S(1)} %get-tuple-element.97), channel_id=1, source_target_pairs={{16,0},{32,16},{48,32},{64,48},{80,64},{96,80},{112,96},{128,112},... | collective-permute-start | bytes 24584 | tf_op jit(solution)/shard_map/ppermute | solution.py:25
  265.3 6.5 %collective-permute-start.47 = (f32[2,1,8,128]{3,2,1,0:T(8,128)S(1)}, f32[2,1,8,128]{3,2,1,0:T(8,128)S(1)}, u32[]{:S(2)}, u32[]{:S(2)}) collective-permute-start(f32[2,1,8,128]{3,2,1,0:T(8,128)S(1)} %get-tuple-element.98), channel_id=1, source_target_pairs={{0,16},{16,32},{32,48},{48,64},{64,80},{80,96},{96,112},{112,128},... | collective-permute-start | bytes 24584 | tf_op jit(solution)/shard_map/ppermute | solution.py:24
  (300 other events, 6427.2 us)
